TPU v7x, 128 devices: a whole 4x4x4 slice. The times are simulated.
128 devices in a mesh: req: 32 (over y, x, core), mlp: 4 (over z).
Axes of the slice: x: 4, y: 4, z: 4, core: 2. Of those that a mesh axis runs over, the one named last changes fastest.
Arguments:
- states: bfloat16 [8192, 2560], P('req')
- attn_gain: float32 [2560], replicated, may hold values from 0.1 to 1.9
- query_matrix: bfloat16 [2560, 2048], P(None, 'mlp')
- key_matrix: bfloat16 [2560, 1024], P(None, 'mlp')
- value_matrix: bfloat16 [2560, 1024], P(None, 'mlp'), may hold values from -0.125 to 0.125
- query_gain: float32 [256], replicated
- key_gain: float32 [256], replicated
- out_weight: bfloat16 [2048, 2560], P('mlp'), may hold values from -0.125 to 0.125
- post_gain: float32 [2560], replicated, may hold values from 0.1 to 1.9
- ffw_gain: float32 [2560], replicated, may hold values from 0.1 to 1.9
- gate_weight: bfloat16 [2560, 10240], P(None, 'req'), may hold values from -0.125 to 0.125
- up_weight: bfloat16 [2560, 10240], P(None, 'req'), may hold values from -0.125 to 0.125
- down_weight: bfloat16 [10240, 2560], P('req'), may hold values from -0.0625 to 0.0625
- post_ffw_gain: float32 [2560], replicated, may hold values from 0.1 to 1.9
- prefix_key_cache: bfloat16 [32, 512, 1024], P('req', None, 'mlp')
- prefix_value_cache: bfloat16 [32, 512, 1024], P('req', None, 'mlp'), may hold values from -6 to 6
- segment: int32 [8192], P('req'), may hold values from 0 to 15, as said below
- prefix_id: int32 [8192], P('req'), may hold values from 0 to 31, as said below
- owner_map: int32 [32], replicated, may hold values from 0 to 31, each once
Outputs:
- layer_out: bfloat16 [8192, 2560], P(('req', 'mlp'))
Inputs may be any that keep to these rules, and one draw needn't show every extreme that they name: Within each block of 256 rows, equal segment values mark one request and occupy contiguous rows; requests hold 16 or 32 tokens. `prefix_id`: all tokens of one request name the same prefix group. In each block of 256 rows at most 32 rows name prefix groups of the same owner, and one prefix group is named by exactly 32 rows of every block.
All inputs are finite; a program needn't handle non-finite values.
Results may differ from a plain program's by a relative error of at most 0.017.
The roundings to bfloat16 on the way count: a program that leaves them out, or rounds other values in their place, can miss the bound.
Values may be sent and summed in bfloat16 or wider, within the bound.
A program may use at most 128 MiB of HBM per device.

v0:
```python
import jax
import jax.numpy as jnp
from jax import lax
from jax.sharding import PartitionSpec as P

CAP = 32


EPS = 1e-06


def normed(values_in, gain_vec):
    return (
        values_in
        * lax.rsqrt(jnp.mean(values_in * values_in, axis=-1, keepdims=True) + EPS)
        * gain_vec
    )


def local_attention(query_rows, key_rows, value_rows, segment_rows, score_scale):
    scores = (
        jnp.einsum("tgqd,sgd->gqts", query_rows, key_rows, preferred_element_type=jnp.float32)
        * score_scale
    )
    row_count = segment_rows.shape[0]
    token_position = jnp.arange(row_count, dtype=jnp.int32)
    allowed = (segment_rows[:, None] == segment_rows[None, :]) & (
        token_position[:, None] >= token_position[None, :]
    )
    scores = jnp.where(allowed, scores, -jnp.inf)
    row_max = jnp.max(scores, axis=-1, keepdims=True)
    powers = jnp.exp(scores - row_max)
    row_sum = jnp.sum(powers, axis=-1, keepdims=True)
    weights = (powers / row_sum).astype(jnp.bfloat16)
    mixed = jnp.einsum("gqts,sgd->tgqd", weights, value_rows, preferred_element_type=jnp.float32)
    log_total = jnp.transpose((row_max + jnp.log(row_sum))[..., 0], (2, 0, 1))
    return (mixed, log_total)


def prefix_partials(incoming, stored_keys, stored_values, score_scale):
    sources, slot_count, head_cols = incoming.shape
    kv_heads = stored_keys.shape[1]
    head_dim = stored_keys.shape[2]
    query_group_width = head_cols // (kv_heads * head_dim)
    query_rows = incoming.reshape(sources * slot_count, kv_heads, query_group_width, head_dim)
    scores = (
        jnp.einsum("rgqd,kgd->rgqk", query_rows, stored_keys, preferred_element_type=jnp.float32)
        * score_scale
    )
    row_max = jnp.max(scores, axis=-1, keepdims=True)
    powers = jnp.exp(scores - row_max)
    row_sum = jnp.sum(powers, axis=-1, keepdims=True)
    weights = (powers / row_sum).astype(jnp.bfloat16)
    mixed = jnp.einsum("rgqk,kgd->rgqd", weights, stored_values, preferred_element_type=jnp.float32)
    mixed = lax.optimization_barrier(mixed.astype(jnp.bfloat16)).astype(jnp.float32)
    log_total = row_max[..., 0] + jnp.log(row_sum[..., 0])
    return (
        mixed.reshape(sources, slot_count, head_cols),
        log_total.reshape(sources, slot_count, kv_heads * query_group_width),
    )


def body(
    states,
    attn_gain,
    query_matrix,
    key_matrix,
    value_matrix,
    query_gain,
    key_gain,
    out_weight,
    post_gain,
    ffw_gain,
    gate_weight,
    up_weight,
    down_weight,
    post_ffw_gain,
    prefix_key_cache,
    prefix_value_cache,
    segment,
    prefix_id,
    owner_map,
):
    row_count = states.shape[0]
    head_dim = query_gain.shape[0]
    kv_heads = key_matrix.shape[1] // head_dim
    head_cols = query_matrix.shape[1]
    query_group_width = head_cols // (kv_heads * head_dim)
    score_scale = head_dim ** (-0.5)
    req_count = lax.axis_size("req")
    mlp_count = lax.axis_size("mlp")
    mlp_index = lax.axis_index("mlp")
    quarter = row_count // mlp_count
    states_f = states.astype(jnp.float32)
    normalized_input = normed(states_f, attn_gain).astype(jnp.bfloat16)
    unnormed_queries = jnp.dot(
        normalized_input, query_matrix, preferred_element_type=jnp.float32
    ).reshape(row_count, kv_heads, query_group_width, head_dim)
    query_vectors = normed(unnormed_queries, query_gain).astype(jnp.bfloat16)
    unnormed_keys = jnp.dot(
        normalized_input, key_matrix, preferred_element_type=jnp.float32
    ).reshape(row_count, kv_heads, head_dim)
    key_vectors = normed(unnormed_keys, key_gain).astype(jnp.bfloat16)
    value_vectors = (
        jnp.dot(normalized_input, value_matrix, preferred_element_type=jnp.float32)
        .astype(jnp.bfloat16)
        .reshape(row_count, kv_heads, head_dim)
    )
    prefix_count = owner_map.shape[0]
    prefix_onehot = (
        prefix_id[:, None] == jnp.arange(prefix_count, dtype=jnp.int32)[None, :]
    ).astype(jnp.int32)
    target = jnp.sum(prefix_onehot * owner_map[None, :], axis=1)
    to_owner = (target[:, None] == jnp.arange(req_count, dtype=jnp.int32)[None, :]).astype(
        jnp.float32
    )
    token_position = jnp.arange(row_count, dtype=jnp.int32)
    earlier = (token_position[:, None] > token_position[None, :]).astype(jnp.float32)
    counts = jnp.dot(earlier, to_owner, precision=lax.Precision.HIGHEST)
    slot_index = jnp.sum(to_owner * counts, axis=1).astype(jnp.int32)
    place_row = target * CAP + slot_index
    placing = (place_row[None, :] == jnp.arange(req_count * CAP, dtype=jnp.int32)[:, None]).astype(
        jnp.bfloat16
    )
    outgoing = (
        jnp.dot(
            placing, query_vectors.reshape(row_count, head_cols), preferred_element_type=jnp.float32
        )
        .astype(jnp.bfloat16)
        .reshape(req_count, CAP, head_cols)
    )
    stored_keys = prefix_key_cache[0].reshape(-1, kv_heads, head_dim)
    stored_values = prefix_value_cache[0].reshape(-1, kv_heads, head_dim)
    suffix_output, suffix_log_sum = local_attention(
        query_vectors, key_vectors, value_vectors, segment, score_scale
    )
    mixed, log_total = prefix_partials(
        lax.all_to_all(outgoing, "req", split_axis=0, concat_axis=0, tiled=True),
        stored_keys,
        stored_values,
        score_scale,
    )
    back_out = lax.all_to_all(
        mixed.astype(jnp.bfloat16), "req", split_axis=0, concat_axis=0, tiled=True
    ).astype(mixed.dtype)
    back_lse = lax.all_to_all(
        log_total.astype(jnp.bfloat16), "req", split_axis=0, concat_axis=0, tiled=True
    ).astype(log_total.dtype)
    prefix_out = back_out.reshape(req_count * CAP, head_cols)[place_row].reshape(
        row_count, kv_heads, query_group_width, head_dim
    )
    prefix_lse = back_lse.reshape(req_count * CAP, kv_heads * query_group_width)[place_row].reshape(
        row_count, kv_heads, query_group_width
    )
    prefix_out, prefix_lse = (prefix_out, prefix_lse)
    blend = jax.nn.sigmoid(prefix_lse - suffix_log_sum)[..., None]
    attended = (
        (blend * prefix_out + (1.0 - blend) * suffix_output)
        .astype(jnp.bfloat16)
        .reshape(row_count, head_cols)
    )
    partial_value = jnp.dot(attended, out_weight, preferred_element_type=jnp.float32)
    full_sum = lax.psum(partial_value.astype(jnp.bfloat16), "mlp").astype(jnp.float32)
    summed = lax.dynamic_slice_in_dim(full_sum, mlp_index * quarter, quarter, 0)
    own_rows = lax.dynamic_slice_in_dim(states_f, mlp_index * quarter, quarter, 0)
    residual = own_rows + normed(summed, post_gain)
    ffw_in = normed(residual, ffw_gain).astype(jnp.bfloat16)
    piece = lax.all_gather(ffw_in, "req", axis=0, tiled=True)
    gate_proj = jnp.dot(piece, gate_weight, preferred_element_type=jnp.float32)
    up_proj = jnp.dot(piece, up_weight, preferred_element_type=jnp.float32)
    hidden = (jax.nn.gelu(gate_proj, approximate=True) * up_proj).astype(jnp.bfloat16)
    down_sum = lax.psum_scatter(
        jnp.dot(hidden, down_weight, preferred_element_type=jnp.float32).astype(jnp.bfloat16),
        "req",
        scatter_dimension=0,
        tiled=True,
    ).astype(jnp.float32)
    return (residual + normed(down_sum, post_ffw_gain)).astype(jnp.bfloat16)


def solution(mesh):
    return jax.shard_map(
        body,
        mesh=mesh,
        in_specs=(
            P("req", None),
            P(),
            P(None, "mlp"),
            P(None, "mlp"),
            P(None, "mlp"),
            P(),
            P(),
            P("mlp", None),
            P(),
            P(),
            P(None, "req"),
            P(None, "req"),
            P("req", None),
            P(),
            P("req", None, "mlp"),
            P("req", None, "mlp"),
            P("req"),
            P("req"),
            P(),
        ),
        out_specs=P(("req", "mlp"), None),
        check_vma=False,
    )
```

profile of v0, /device:TPU:0, one launch (start us, length us, event | category | flops | bytes accessed | tf_op | source)
XLA Modules:
  0.0 342.5 jit_solution(14212697419758735946)
XLA Ops:
  10.0 4.1 %fusion.66 = (f32[256,512]{1,0:T(8,128)}, f32[256,512]{1,0:T(8,128)}) fusion(bf16[2560,512]{1,0:T(8,128)(2,1)} %param.21, f32[2560]{0:T(1024)} %param.20, f32[256]{0:T(256)S(1)} %add_rsqrt_fusion.2, bf16[256,2560]{1,0:T(8,128)(2,1)} %param.19), kind=kOutput, calls=%fused_computation.108 | convolution fusion | flops 673841152 | bytes 4992000 | tf_op jit(solution)/shard_map/dot_general | solution.py:96
  18.9 7.5 %all-to-all-start = ((bf16[32,32,512]{2,1,0:T(8,128)(2,1)}), bf16[32,32,512]{2,1,0:T(8,128)(2,1)}, u32[]{:S(2)}, u32[]{:S(2)}) async-start(bf16[32,32,512]{2,1,0:T(8,128)(2,1)} %bitcast.130), calls=%async_computation | async-start | bytes 2097152 | tf_op jit(solution)/shard_map/all_to_all | solution.py:138
  26.6 3.2 multiply_reduce_fusion.2
  29.8 13.9 %all-to-all-done = bf16[32,32,512]{2,1,0:T(8,128)(2,1)} async-done(((bf16[32,32,512]{2,1,0:T(8,128)(2,1)}), bf16[32,32,512]{2,1,0:T(8,128)(2,1)}, u32[]{:S(2)}, u32[]{:S(2)}) %all-to-all-start) | async-done | bytes 1048608 | tf_op jit(solution)/shard_map/all_to_all | solution.py:138
  43.8 2.2 reshape.279
  46.0 2.0 bitcast_reduce_fusion
  51.3 3.8 %all-to-all-start.1 = ((bf16[32,32,2]{1,2,0:T(2,128)(2,1)}), bf16[32,32,2]{1,2,0:T(2,128)(2,1)S(1)}, u32[]{:S(2)}, u32[]{:S(2)}) async-start(bf16[32,32,2]{1,2,0:T(2,128)(2,1)} %copy.99), calls=%async_computation.1 | async-start | bytes 32768 | tf_op jit(solution)/shard_map/all_to_all | solution.py:146
  55.1 3.5 %fusion.16 = bf16[1024,1,2,256]{3,0,2,1:T(8,128)(2,1)S(1)} fusion(f32[1024,2]{0,1:T(2,128)S(1)} %fusion.1, f32[1024,2]{0,1:T(2,128)S(1)} %get-tuple-element.9, f32[1024,2,512]{0,2,1:T(8,128)} %copy-done.1, bf16[1,512,256]{2,1,0:T(8,128)(2,1)S(1)} %copy-done.8), kind=kOutput, calls=%fused_computation.26 | convolution fusion | flops 541589504 | bytes 5521408 | tf_op jit(solution)/shard_map/rgqk,kgd->rgqd/dot_general | solution.py:54
  58.6 2.1 copy.106
  60.7 2.6 convert_element_type.114
  63.3 7.5 %all-to-all-start.2 = ((bf16[32,32,512]{2,1,0:T(8,128)(2,1)}), bf16[32,32,512]{2,1,0:T(8,128)(2,1)}, u32[]{:S(2)}, u32[]{:S(2)}) async-start(bf16[32,32,512]{2,1,0:T(8,128)(2,1)} %convert_element_type.114), calls=%async_computation.2 | async-start | bytes 2097152 | tf_op jit(solution)/shard_map/all_to_all | solution.py:143
  73.4 14.8 %all-to-all-done.2 = bf16[32,32,512]{2,1,0:T(8,128)(2,1)} async-done(((bf16[32,32,512]{2,1,0:T(8,128)(2,1)}), bf16[32,32,512]{2,1,0:T(8,128)(2,1)}, u32[]{:S(2)}, u32[]{:S(2)}) %all-to-all-start.2) | async-done | bytes 1048608 | tf_op jit(solution)/shard_map/all_to_all | solution.py:143
  88.1 2.9 bitcast_convert_fusion
  91.0 2.8 gather_fusion.1
  94.8 2.9 fusion.26
  97.7 1.9 convolution_convert_fusion.1
  99.7 3.2 convert_element_type.100
  102.9 43.6 %all-reduce.2.cloned.1.call-done = bf16[256,2560]{1,0:T(8,128)(2,1)} async-done(((bf16[256,2560]{1,0:T(8,128)(2,1)}), bf16[256,2560]{1,0:T(8,128)(2,1)}) %all-reduce.2.cloned.1.call-update) | async-done | bytes 1310736 | tf_op jit(solution)/shard_map/psum | solution.py:163
  149.2 2.1 multiply_convert_fusion.1
  151.4 58.3 %all-gather.2.cloned.1.call-done = bf16[2048,2560]{1,0:T(8,128)(2,1)} async-done(((bf16[64,2560]{1,0:T(8,128)(2,1)}), bf16[2048,2560]{1,0:T(8,128)(2,1)}) %all-gather.2.cloned.1.call-update) | async-done | bytes 10485776 | tf_op jit(solution)/shard_map/all_gather | solution.py:168
  209.7 9.5 %fusion.68 = f32[2048,320]{0,1:T(8,128)} fusion(bf16[2048,2560]{1,0:T(8,128)(2,1)} %all-gather.2.cloned.1.call-done, bf16[2560,320]{0,1:T(8,128)(2,1)} %param.29), kind=kOutput, calls=%fused_computation.110 | convolution fusion | flops 3355443200 | bytes 14745600 | tf_op jit(solution)/shard_map/dot_general | solution.py:169
  219.2 15.6 %convolution_convert_fusion = bf16[2048,2560]{1,0:T(8,128)(2,1)} fusion(bf16[320,2560]{1,0:T(8,128)(2,1)} %param.31, bf16[2048,2560]{1,0:T(8,128)(2,1)} %all-gather.2.cloned.1.call-done, bf16[2560,320]{0,1:T(8,128)(2,1)} %param.30, f32[2048,320]{0,1:T(8,128)} %fusion.68), kind=kOutput, calls=%fused_computation.2 | convolution fusion | flops 6722682880 | bytes 26869760 | tf_op jit(solution)/shard_map/dot_general | solution.py:173
  234.9 97.7 %reduce-scatter.2.cloned.1.call-done = bf16[64,2560]{1,0:T(8,128)(2,1)} async-done(((bf16[2048,2560]{1,0:T(8,128)(2,1)}), bf16[64,2560]{1,0:T(8,128)(2,1)}) %reduce-scatter.2.cloned.1.call-update) | async-done | bytes 327696 | tf_op jit(solution)/shard_map/reduce_scatter | solution.py:172
  333.7 2.3 fusion.38
  (69 shorter events, 19.1 us)
Async XLA Ops:
  6.5 91.2 %copy-start = (bf16[512,2560]{1,0:T(8,128)(2,1)S(1)}, bf16[512,2560]{1,0:T(8,128)(2,1)}, u32[]{:S(2)}) copy-start(bf16[512,2560]{1,0:T(8,128)(2,1)} %param.26) | copy-start | bytes 7864324
  16.2 10.2 %copy-start.7 = (s32[256]{0:T(256)S(1)}, s32[256]{0:T(256)}, u32[]{:S(2)}) copy-start(s32[256]{0:T(256)} %param.35) | copy-start | bytes 3076
  16.3 10.3 %copy-start.9 = (f32[2560]{0:T(1024)S(1)}, f32[2560]{0:T(1024)}, u32[]{:S(2)}) copy-start(f32[2560]{0:T(1024)} %param.20) | copy-start | bytes 30724
  18.9 24.9 %all-to-all-start = ((bf16[32,32,512]{2,1,0:T(8,128)(2,1)}), bf16[32,32,512]{2,1,0:T(8,128)(2,1)}, u32[]{:S(2)}, u32[]{:S(2)}) async-start(bf16[32,32,512]{2,1,0:T(8,128)(2,1)} %bitcast.130), calls=%async_computation | async-start | bytes 2097152 | tf_op jit(solution)/shard_map/all_to_all | solution.py:138
  26.6 19.4 %copy-start.3 = (bf16[1,512,256]{2,1,0:T(8,128)(2,1)S(1)}, bf16[1,512,256]{2,1,0:T(8,128)(2,1)}, u32[]{:S(2)}) copy-start(bf16[1,512,256]{2,1,0:T(8,128)(2,1)} %param.33) | copy-start | bytes 786436
  48.0 1.9 copy-start.1
  48.0 7.1 %copy-start.8 = (bf16[1,512,256]{2,1,0:T(8,128)(2,1)S(1)}, bf16[1,512,256]{2,1,0:T(8,128)(2,1)}, u32[]{:S(2)}) copy-start(bf16[1,512,256]{2,1,0:T(8,128)(2,1)} %param.34) | copy-start | bytes 786436
  51.3 12.0 %all-to-all-start.1 = ((bf16[32,32,2]{1,2,0:T(2,128)(2,1)}), bf16[32,32,2]{1,2,0:T(2,128)(2,1)S(1)}, u32[]{:S(2)}, u32[]{:S(2)}) async-start(bf16[32,32,2]{1,2,0:T(2,128)(2,1)} %copy.99), calls=%async_computation.1 | async-start | bytes 32768 | tf_op jit(solution)/shard_map/all_to_all | solution.py:146
  60.7 10.3 %copy-start.11 = (f32[256]{0:T(256)S(1)}, f32[256]{0:T(256)}, u32[]{:S(2)}) copy-start(f32[256]{0:T(256)} %param.25) | copy-start | bytes 3076
  60.7 10.3 %copy-start.12 = (f32[256,256]{0,1:T(8,128)S(1)}, f32[256,256]{0,1:T(8,128)}, u32[]{:S(2)}) copy-start(f32[256,256]{0,1:T(8,128)} %get-tuple-element.12) | copy-start | bytes 786436
  63.3 24.8 %all-to-all-start.2 = ((bf16[32,32,512]{2,1,0:T(8,128)(2,1)}), bf16[32,32,512]{2,1,0:T(8,128)(2,1)}, u32[]{:S(2)}, u32[]{:S(2)}) async-start(bf16[32,32,512]{2,1,0:T(8,128)(2,1)} %convert_element_type.114), calls=%async_computation.2 | async-start | bytes 2097152 | tf_op jit(solution)/shard_map/all_to_all | solution.py:143
  70.8 75.7 %all-reduce.2.cloned.1.call-start = ((), (), s32[]{:S(2)}) async-start(), calls=%async_computation.4 | async-start | bytes 2621440 | tf_op jit(solution)/shard_map/psum | solution.py:163
  71.4 0.8 copy-start.2
  91.0 3.8 %copy-start.10 = (f32[2560]{0:T(1024)S(1)}, f32[2560]{0:T(1024)}, u32[]{:S(2)}) copy-start(f32[2560]{0:T(1024)} %param.20) | copy-start | bytes 30724
  99.6 48.0 %copy-start.4 = (f32[2560]{0:T(1024)S(1)}, f32[2560]{0:T(1024)}, u32[]{:S(2)}) copy-start(f32[2560]{0:T(1024)} %param.27) | copy-start | bytes 30724
  99.7 110.0 %all-gather.2.cloned.1.call-start = ((), (), s32[]{:S(2)}) async-start(), calls=%async_computation.5 | async-start | bytes 10813440 | tf_op jit(solution)/shard_map/all_gather | solution.py:168
  99.7 49.4 %copy-start.5 = (f32[2560]{0:T(1024)S(1)}, f32[2560]{0:T(1024)}, u32[]{:S(2)}) copy-start(f32[2560]{0:T(1024)} %param.28) | copy-start | bytes 30724
  151.3 181.2 %reduce-scatter.2.cloned.1.call-start = ((), (), s32[]{:S(2)}) async-start(), calls=%async_computation.6 | async-start | bytes 10813440 | tf_op jit(solution)/shard_map/reduce_scatter | solution.py:172
  234.8 98.9 %copy-start.6 = (f32[2560]{0:T(1024)S(1)}, f32[2560]{0:T(1024)}, u32[]{:S(2)}) copy-start(f32[2560]{0:T(1024)} %param.32) | copy-start | bytes 30724
Sparse Core Ops, SparseCore 0:
  99.8 46.6 all-reduce.1
  151.5 58.1 all-gather.1
  235.0 97.5 reduce-scatter.1
where the time goes:
time: 343 us
  waiting for transfers between devices  228 us (66%)
  matrix products  44.8 us (13%)
  other arithmetic  19.4 us (6%)
  starting transfers between devices  19.1 us (6%)
  local copies, waits for them, and re-layouts  17.5 us (5%)
  between operations  13.4 us (4%)
    reduce_scatter x1, waiting for transfers between devices, body(): lax.psum_scatter(jnp.dot(hidden, down_weight, preferred_element_type=jnp....  97.7 us
    all_gather x1, waiting for transfers between devices, body(): piece = lax.all_gather(ffw_in, 'req', axis=0, tiled=True)  58.3 us
    psum x1, waiting for transfers between devices, body(): lax.psum(partial_value.astype(jnp.bfloat16), 'mlp').astype(jnp.float32)  43.6 us
    dot_general x1, matrix products, body(): jnp.dot(hidden, down_weight, preferred_element_type=jnp.float32)  15.6 us
    all_to_all x1, waiting for transfers between devices, body(): lax.all_to_all(mixed.astype(jnp.bfloat16), 'req', split_axis=0, concat_ax...  14.8 us
    all_to_all x1, waiting for transfers between devices, body(): lax.all_to_all(outgoing, 'req', split_axis=0, concat_axis=0, tiled=True)  13.9 us
    dot_general x1, matrix products, body(): gate_proj = jnp.dot(piece, gate_weight, preferred_element_type=jnp.float32)  9.52 us
    all_to_all x1, starting transfers between devices, body(): lax.all_to_all(outgoing, 'req', split_axis=0, concat_axis=0, tiled=True)  7.53 us
  transfers between devices with their start and end apart: 6, of which 5 were waited for; matrix products, arithmetic and copies ran while one was open for 5% of the time, Pallas kernels for 0%

commit v1 on v0

--- a/solution.py
+++ b/solution.py
@@ -1,6 +1,8 @@
 import jax
 import jax.numpy as jnp
 from jax import lax
+from jax.experimental import pallas as pl
+from jax.experimental.pallas import tpu as pltpu
 from jax.sharding import PartitionSpec as P
 
 CAP = 32
@@ -58,6 +60,335 @@
         mixed.reshape(sources, slot_count, head_cols),
         log_total.reshape(sources, slot_count, kv_heads * query_group_width),
     )
+
+
+MESH_ID = pl.DeviceIdType.MESH
+RING = 4
+SUB = 32
+HALF = 16
+
+
+def torus_place():
+    me = lax.axis_index("req")
+    layer = lax.axis_index("mlp")
+    core = lax.rem(me, 2)
+    chip = me // 2
+    col = lax.rem(chip, RING)
+    row = chip // RING
+
+    def at(row_at, col_at, core_at):
+        return ((row_at * RING + col_at) * 2 + core_at, layer)
+
+    up = at(lax.rem(row + 1, RING), col, core)
+    down = at(lax.rem(row + RING - 1, RING), col, core)
+    right = at(row, lax.rem(col + 1, RING), core)
+    left = at(row, lax.rem(col + RING - 1, RING), core)
+    sibling = at(row, col, 1 - core)
+    return right, left, up, down, sibling
+
+
+def ffn_kernel(
+    ffw_in_ref,
+    residual_ref,
+    gain_ref,
+    gate_ref,
+    up_ref,
+    down_ref,
+    out_ref,
+    rows_buf,
+    gate_up,
+    down_w,
+    partial,
+    opposite_in,
+    merged_out,
+    side_in,
+    row_sum,
+    opposite_in2,
+    send2,
+    merged_out2,
+    side_in2,
+    local_sem,
+    send_sem,
+    recv_sem,
+    weight_send,
+    weight_recv,
+):
+    right, left, upper, lower, sibling = torus_place()
+    hidden = gate_ref.shape[0]
+    barrier = pltpu.get_barrier_semaphore()
+    for peer in (right, left, upper, lower, sibling):
+        pl.semaphore_signal(barrier, inc=1, device_id=peer, device_id_type=MESH_ID)
+
+    first = ((right, left), (upper, lower))
+    second = ((upper, lower), (right, left))
+    copies = []
+    count = [0]
+
+    def send(src, dst, peer):
+        index = count[0]
+        count[0] += 1
+        copy = pltpu.make_async_remote_copy(
+            src_ref=src,
+            dst_ref=dst,
+            send_sem=send_sem.at[index],
+            recv_sem=recv_sem.at[index],
+            device_id=peer,
+            device_id_type=MESH_ID,
+        )
+        copy.start()
+        copies.append(copy)
+        return copy
+
+    local = []
+    sources = (gate_ref, up_ref, down_ref)
+    targets = (
+        gate_up.at[pl.ds(0, hidden)],
+        gate_up.at[pl.ds(2 * hidden, hidden)],
+        down_w.at[pl.ds(0, hidden)],
+    )
+    far_targets = (
+        gate_up.at[pl.ds(hidden, hidden)],
+        gate_up.at[pl.ds(3 * hidden, hidden)],
+        down_w.at[pl.ds(hidden, hidden)],
+    )
+    for index, (src, dst) in enumerate(zip(sources, targets)):
+        copy = pltpu.make_async_copy(src, dst, local_sem.at[index])
+        copy.start()
+        local.append(copy)
+
+    def slot(group, chunk, sub, start=0, size=SUB):
+        return rows_buf.at[chunk, pl.ds(group * RING * SUB + sub * SUB + start, size)]
+
+    for group in range(2):
+        rows_buf[0, pl.ds(group * RING * SUB, SUB)] = ffw_in_ref[pl.ds(group * SUB, SUB)]
+    pl.semaphore_wait(barrier, 5)
+
+    step1 = []
+    for group in range(2):
+        plus, minus = first[group]
+        step1.append(
+            (
+                send(slot(group, 0, 0), slot(group, 0, 3), plus),
+                send(slot(group, 0, 0), slot(group, 0, 1), minus),
+            )
+        )
+    across = {}
+
+    def send_across(group, sub):
+        plus, minus = second[group]
+        across[group, sub] = (
+            send(slot(group, 0, sub), slot(group, 3, sub), plus),
+            send(slot(group, 0, sub), slot(group, 1, sub), minus),
+        )
+
+    relays = {}
+
+    def relay_across(group, sub):
+        plus, minus = second[group]
+        across[group, sub][0].wait_recv()
+        a = send(slot(group, 3, sub, 0, HALF), slot(group, 2, sub, 0, HALF), plus)
+        across[group, sub][1].wait_recv()
+        b = send(slot(group, 1, sub, HALF, HALF), slot(group, 2, sub, HALF, HALF), minus)
+        relays[group, sub] = (a, b)
+
+    for group in range(2):
+        send_across(group, 0)
+    weight_copies = []
+    for index, (src, dst) in enumerate(zip(sources, far_targets)):
+        copy = pltpu.make_async_remote_copy(
+            src_ref=src,
+            dst_ref=dst,
+            send_sem=weight_send.at[index],
+            recv_sem=weight_recv.at[index],
+            device_id=sibling,
+            device_id_type=MESH_ID,
+        )
+        copy.start()
+        weight_copies.append(copy)
+    step2 = []
+    for group in range(2):
+        plus, minus = first[group]
+        step1[group][0].wait_recv()
+        a = send(slot(group, 0, 3, 0, HALF), slot(group, 0, 2, 0, HALF), plus)
+        step1[group][1].wait_recv()
+        b = send(slot(group, 0, 1, HALF, HALF), slot(group, 0, 2, HALF, HALF), minus)
+        step2.append((a, b))
+    for group in range(2):
+        send_across(group, 1)
+        send_across(group, 3)
+    for group in range(2):
+        relay_across(group, 0)
+    for group in range(2):
+        step2[group][0].wait_recv()
+        step2[group][1].wait_recv()
+        send_across(group, 2)
+
+    for copy in local:
+        copy.wait()
+    for copy in weight_copies:
+        copy.wait_recv()
+
+    def compute(chunk):
+        rows = rows_buf[chunk]
+        both = lax.dot_general(
+            rows, gate_up[...], (((1,), (1,)), ((), ())), preferred_element_type=jnp.float32
+        )
+        gate = both[:, : 2 * hidden]
+        act = (jax.nn.gelu(gate, approximate=True) * both[:, 2 * hidden :]).astype(jnp.bfloat16)
+        partial[chunk] = jnp.dot(act, down_w[...], preferred_element_type=jnp.float32).astype(
+            jnp.bfloat16
+        )
+
+    for group in range(2):
+        relay_across(group, 1)
+        relay_across(group, 3)
+    compute(0)
+    for group in range(2):
+        relay_across(group, 2)
+    compute(1)
+
+    span = RING * SUB
+    half = span // 2
+
+    def part(buf, group, chunk, which):
+        return buf.at[chunk, pl.ds(group * span + which * half, half)]
+
+    def side(group, which, low):
+        return side_in.at[which, pl.ds(group * span + low * half, half)]
+
+    plain = []
+    for group in range(2):
+        plus, minus = second[group]
+        plain.append([send(part(partial, group, 1, 1), side(group, 0, 1), plus)])
+    compute(3)
+    for group in range(2):
+        plus, minus = second[group]
+        plain[group].append(send(part(partial, group, 3, 0), side(group, 1, 0), minus))
+    for pair in relays.values():
+        pair[0].wait_recv()
+        pair[1].wait_recv()
+    compute(2)
+    opposite = []
+    for group in range(2):
+        plus, minus = second[group]
+        opposite.append(
+            (
+                send(part(partial, group, 2, 0), opposite_in.at[0, pl.ds(group * half, half)], plus),
+                send(part(partial, group, 2, 1), opposite_in.at[1, pl.ds(group * half, half)], minus),
+            )
+        )
+    merged = []
+    for group in range(2):
+        plus, minus = second[group]
+        rows = pl.ds(group * half, half)
+        opposite[group][0].wait_recv()
+        merged_out[0, rows] = (
+            part(partial, group, 1, 0)[...].astype(jnp.float32)
+            + opposite_in[0, rows].astype(jnp.float32)
+        ).astype(jnp.bfloat16)
+        a = send(merged_out.at[0, rows], side(group, 0, 0), plus)
+        opposite[group][1].wait_recv()
+        merged_out[1, rows] = (
+            part(partial, group, 3, 1)[...].astype(jnp.float32)
+            + opposite_in[1, rows].astype(jnp.float32)
+        ).astype(jnp.bfloat16)
+        b = send(merged_out.at[1, rows], side(group, 1, 1), minus)
+        merged.append((a, b))
+
+    def summed(group, sub):
+        rows = pl.ds(group * span + sub * SUB, SUB)
+        return (
+            partial[0, rows].astype(jnp.float32)
+            + side_in[0, rows].astype(jnp.float32)
+            + side_in[1, rows].astype(jnp.float32)
+        )
+
+    last = []
+    for group in range(2):
+        plus, minus = first[group]
+        plain[group][0].wait_recv()
+        merged[group][1].wait_recv()
+        send2[group, 2] = summed(group, 2).astype(jnp.bfloat16)
+        a = send(send2.at[group, 2, pl.ds(0, HALF)], opposite_in2.at[group, 0], plus)
+        b = send(send2.at[group, 2, pl.ds(HALF, HALF)], opposite_in2.at[group, 1], minus)
+        last.append([a, b])
+    for group in range(2):
+        plus, minus = first[group]
+        plain[group][1].wait_recv()
+        merged[group][0].wait_recv()
+        row_sum[group, 0] = summed(group, 1)
+        row_sum[group, 1] = summed(group, 3)
+        send2[group, 1] = row_sum[group, 0].astype(jnp.bfloat16)
+        send2[group, 3] = row_sum[group, 1].astype(jnp.bfloat16)
+        a = send(
+            send2.at[group, 1, pl.ds(HALF, HALF)], side_in2.at[group, 0, pl.ds(HALF, HALF)], plus
+        )
+        b = send(send2.at[group, 3, pl.ds(0, HALF)], side_in2.at[group, 1, pl.ds(0, HALF)], minus)
+        last[group] += [a, b]
+    for group in range(2):
+        plus, minus = first[group]
+        last[group][0].wait_recv()
+        merged_out2[group, 0] = (
+            row_sum[group, 0, pl.ds(0, HALF)] + opposite_in2[group, 0].astype(jnp.float32)
+        ).astype(jnp.bfloat16)
+        a = send(merged_out2.at[group, 0], side_in2.at[group, 0, pl.ds(0, HALF)], plus)
+        last[group][1].wait_recv()
+        merged_out2[group, 1] = (
+            row_sum[group, 1, pl.ds(HALF, HALF)] + opposite_in2[group, 1].astype(jnp.float32)
+        ).astype(jnp.bfloat16)
+        b = send(merged_out2.at[group, 1], side_in2.at[group, 1, pl.ds(HALF, HALF)], minus)
+        last[group] += [a, b]
+    for group in range(2):
+        own = summed(group, 0)
+        for index in (2, 3, 4, 5):
+            last[group][index].wait_recv()
+        total = own + side_in2[group, 0].astype(jnp.float32) + side_in2[group, 1].astype(jnp.float32)
+        rows = pl.ds(group * SUB, SUB)
+        out_ref[rows] = (residual_ref[rows] + normed(total, gain_ref[...])).astype(out_ref.dtype)
+
+    for copy in copies:
+        copy.wait_send()
+    for copy in weight_copies:
+        copy.wait_send()
+
+
+def ffn_block(ffw_in, residual, gain, gate_t, up_t, down_weight):
+    rows, width = ffw_in.shape
+    hidden = gate_t.shape[0]
+    vmem = pl.BlockSpec(memory_space=pltpu.VMEM)
+    hbm = pl.BlockSpec(memory_space=pl.ANY)
+    bf16 = jnp.bfloat16
+    span = RING * SUB
+    copies = 64
+    return pl.pallas_call(
+        ffn_kernel,
+        out_shape=jax.ShapeDtypeStruct((rows, width), bf16),
+        in_specs=[vmem, vmem, vmem, hbm, hbm, hbm],
+        out_specs=vmem,
+        scratch_shapes=[
+            pltpu.VMEM((RING, 2 * span, width), bf16),
+            pltpu.VMEM((4 * hidden, width), bf16),
+            pltpu.VMEM((2 * hidden, width), bf16),
+            pltpu.VMEM((RING, 2 * span, width), bf16),
+            pltpu.VMEM((2, span, width), bf16),
+            pltpu.VMEM((2, span, width), bf16),
+            pltpu.VMEM((2, 2 * span, width), bf16),
+            pltpu.VMEM((2, 2, SUB, width), jnp.float32),
+            pltpu.VMEM((2, 2, HALF, width), bf16),
+            pltpu.VMEM((2, RING, SUB, width), bf16),
+            pltpu.VMEM((2, 2, HALF, width), bf16),
+            pltpu.VMEM((2, 2, SUB, width), bf16),
+            pltpu.SemaphoreType.DMA((3,)),
+            pltpu.SemaphoreType.DMA((copies,)),
+            pltpu.SemaphoreType.DMA((copies,)),
+            pltpu.SemaphoreType.DMA((3,)),
+            pltpu.SemaphoreType.DMA((3,)),
+        ],
+        compiler_params=pltpu.CompilerParams(
+            collective_id=0, has_side_effects=True, vmem_limit_bytes=58 << 20
+        ),
+        name="ffn_block",
+    )(ffw_in, residual, gain, gate_t, up_t, down_weight)
 
 
 def body(
@@ -165,17 +496,9 @@
     own_rows = lax.dynamic_slice_in_dim(states_f, mlp_index * quarter, quarter, 0)
     residual = own_rows + normed(summed, post_gain)
     ffw_in = normed(residual, ffw_gain).astype(jnp.bfloat16)
-    piece = lax.all_gather(ffw_in, "req", axis=0, tiled=True)
-    gate_proj = jnp.dot(piece, gate_weight, preferred_element_type=jnp.float32)
-    up_proj = jnp.dot(piece, up_weight, preferred_element_type=jnp.float32)
-    hidden = (jax.nn.gelu(gate_proj, approximate=True) * up_proj).astype(jnp.bfloat16)
-    down_sum = lax.psum_scatter(
-        jnp.dot(hidden, down_weight, preferred_element_type=jnp.float32).astype(jnp.bfloat16),
-        "req",
-        scatter_dimension=0,
-        tiled=True,
-    ).astype(jnp.float32)
-    return (residual + normed(down_sum, post_ffw_gain)).astype(jnp.bfloat16)
+    return ffn_block(
+        ffw_in, residual, post_ffw_gain[None], gate_weight.T, up_weight.T, down_weight
+    )
 
 
 def solution(mesh):

time: 343 us -> 228 us (0.66)
  waiting for transfers between devices: 228 us -> 71.8 us
  Pallas kernels: 0 us -> 68.9 us
  matrix products: 44.8 us -> 19.7 us
  other arithmetic: 19.4 us -> 14 us
    reduce_scatter x1 -> x0, waiting for transfers between devices: 97.7 us -> none  [body(): lax.psum_scatter(jnp.dot(hidden, down_weight, preferred_element_type=jnp....]
    pallas_call x0 -> x1, Pallas kernels: none -> 68.9 us  [ffn_block(): pl.pallas_call(ffn_kernel, out_shape=jax.ShapeDtypeStruct((rows, width),...]
    all_gather x1 -> x0, waiting for transfers between devices: 58.3 us -> none  [body(): piece = lax.all_gather(ffw_in, 'req', axis=0, tiled=True)]
    dot_general x2 -> x0, matrix products: 25.1 us -> none  [the longest x1 15.6 us: body(): jnp.dot(hidden, down_weight, preferred_element_type=jnp.float32)]
  transfers between devices with their start and end apart: 6 -> 4, of which waited for: 5 -> 3; matrix products, arithmetic and copies ran while one was open for 5% -> 7% of each run, Pallas kernels for 0% -> 0%
where the time goes in v1:
time: 228 us; the launch traced here: 226 us
  waiting for transfers between devices  71.8 us (31%)
  Pallas kernels  68.9 us (30%)
  matrix products  19.7 us (9%)
  local copies, waits for them, and re-layouts  19.2 us (8%)
  starting transfers between devices  19 us (8%)
  other arithmetic  14 us (6%)
  between operations  13.8 us (6%)
    pallas_call x1, Pallas kernels, ffn_block(): pl.pallas_call(ffn_kernel, out_shape=jax.ShapeDtypeStruct((rows, width),...  68.9 us
    psum x1, waiting for transfers between devices, body(): lax.psum(partial_value.astype(jnp.bfloat16), 'mlp').astype(jnp.float32)  43.1 us
    all_to_all x1, waiting for transfers between devices, body(): lax.all_to_all(mixed.astype(jnp.bfloat16), 'req', split_axis=0, concat_ax...  14.8 us
    all_to_all x1, waiting for transfers between devices, body(): lax.all_to_all(outgoing, 'req', split_axis=0, concat_axis=0, tiled=True)  13.9 us
    all_to_all x1, starting transfers between devices, body(): lax.all_to_all(outgoing, 'req', split_axis=0, concat_axis=0, tiled=True)  7.53 us
    all_to_all x1, starting transfers between devices, body(): lax.all_to_all(mixed.astype(jnp.bfloat16), 'req', split_axis=0, concat_ax...  7.47 us
    reduce_sum x4, other arithmetic, normed(): jnp.mean(values_in * values_in, axis=-1, keepdims=True) + EPS  4.78 us
  transfers between devices with their start and end apart: 4, of which 3 were waited for; matrix products, arithmetic and copies ran while one was open for 7% of the time, Pallas kernels for 0%

profile of v1, /device:TPU:0, one launch (start us, length us, event | category | flops | bytes accessed | tf_op | source)
XLA Modules:
  0.0 226.4 jit_solution(5908875091772674284)
XLA Ops:
  6.5 1.8 multiply_reduce_fusion
  8.3 4.1 %fusion.47 = (f32[256,512]{1,0:T(8,128)}, f32[256,512]{1,0:T(8,128)}) fusion(bf16[2560,512]{1,0:T(8,128)(2,1)} %param.21, f32[2560]{0:T(1024)} %param.20, f32[256]{0:T(256)S(1)} %add_rsqrt_fusion.2, bf16[256,2560]{1,0:T(8,128)(2,1)} %param.19), kind=kOutput, calls=%fused_computation.82 | convolution fusion | flops 673841152 | bytes 4992000 | tf_op jit(solution)/shard_map/dot_general | solution.py:427
  16.1 1.5 convolution_convert_fusion.1
  17.6 7.5 %all-to-all-start = ((bf16[32,32,512]{2,1,0:T(8,128)(2,1)}), bf16[32,32,512]{2,1,0:T(8,128)(2,1)}, u32[]{:S(2)}, u32[]{:S(2)}) async-start(bf16[32,32,512]{2,1,0:T(8,128)(2,1)} %bitcast.127), calls=%async_computation | async-start | bytes 2097152 | tf_op jit(solution)/shard_map/all_to_all | solution.py:469
  25.3 3.2 %multiply_reduce_fusion.2 = (f32[256]{0:T(256)S(1)}, f32[256,256]{0,1:T(8,128)}) fusion(bf16[2560,256]{1,0:T(8,128)(2,1)} %param.22, f32[2560]{0:T(1024)S(1)} %copy-done.13, f32[256]{0:T(256)S(1)} %add_rsqrt_fusion.2, bf16[256,2560]{1,0:T(8,128)(2,1)} %param.19), kind=kOutput, calls=%fused_computation.50 | convolution fusion | flops 338296576 | bytes 2895872 | tf_op jit(solution)/shard_map/dot_general | solution.py:431
  28.6 13.9 %all-to-all-done = bf16[32,32,512]{2,1,0:T(8,128)(2,1)} async-done(((bf16[32,32,512]{2,1,0:T(8,128)(2,1)}), bf16[32,32,512]{2,1,0:T(8,128)(2,1)}, u32[]{:S(2)}, u32[]{:S(2)}) %all-to-all-start) | async-done | bytes 1048608 | tf_op jit(solution)/shard_map/all_to_all | solution.py:469
  42.5 2.2 reshape.270
  44.7 2.0 bitcast_reduce_fusion
  46.7 1.9 copy-done.1
  50.0 3.8 %all-to-all-start.1 = ((bf16[32,32,2]{1,2,0:T(2,128)(2,1)}), bf16[32,32,2]{1,2,0:T(2,128)(2,1)S(1)}, u32[]{:S(2)}, u32[]{:S(2)}) async-start(bf16[32,32,2]{1,2,0:T(2,128)(2,1)} %copy.99), calls=%async_computation.1 | async-start | bytes 32768 | tf_op jit(solution)/shard_map/all_to_all | solution.py:477
  53.8 3.5 %fusion.8 = bf16[1024,1,2,256]{3,0,2,1:T(8,128)(2,1)S(1)} fusion(f32[1024,2]{0,1:T(2,128)S(1)} %fusion.1, f32[1024,2]{0,1:T(2,128)S(1)} %get-tuple-element.11, f32[1024,2,512]{0,2,1:T(8,128)} %copy-done.1, bf16[1,512,256]{2,1,0:T(8,128)(2,1)S(1)} %copy-done.12), kind=kOutput, calls=%fused_computation.15 | convolution fusion | flops 541589504 | bytes 5521408 | tf_op jit(solution)/shard_map/rgqk,kgd->rgqd/dot_general | solution.py:56
  57.3 2.1 copy.106
  59.4 2.6 %convert_element_type.102 = bf16[32,32,512]{2,1,0:T(8,128)(2,1)} reshape(bf16[1024,1,2,256]{3,2,0,1:T(2,128)(2,1)} %copy.106) | data formatting | bytes 2097152 | tf_op jit(solution)/shard_map/convert_element_type | solution.py:475
  62.0 7.5 %all-to-all-start.2 = ((bf16[32,32,512]{2,1,0:T(8,128)(2,1)}), bf16[32,32,512]{2,1,0:T(8,128)(2,1)}, u32[]{:S(2)}, u32[]{:S(2)}) async-start(bf16[32,32,512]{2,1,0:T(8,128)(2,1)} %convert_element_type.102), calls=%async_computation.2 | async-start | bytes 2097152 | tf_op jit(solution)/shard_map/all_to_all | solution.py:474
  72.0 14.8 %all-to-all-done.2 = bf16[32,32,512]{2,1,0:T(8,128)(2,1)} async-done(((bf16[32,32,512]{2,1,0:T(8,128)(2,1)}), bf16[32,32,512]{2,1,0:T(8,128)(2,1)}, u32[]{:S(2)}, u32[]{:S(2)}) %all-to-all-start.2) | async-done | bytes 1048608 | tf_op jit(solution)/shard_map/all_to_all | solution.py:474
  86.8 2.9 %bitcast_convert_fusion = f32[1024,512]{1,0:T(8,128)} fusion(bf16[32,32,512]{2,1,0:T(8,128)(2,1)} %all-to-all-done.2), kind=kLoop, calls=%fused_computation.27 | loop fusion | flops 524288 | bytes 3145728 | tf_op jit(solution)/shard_map/reshape | solution.py:480
  89.7 2.8 %gather_fusion.1 = f32[256,512]{1,0:T(8,128)S(1)} fusion(f32[1024,512]{1,0:T(8,128)} %bitcast_convert_fusion, s32[1024]{0:T(1024)S(1)} %pad_clamp_fusion), kind=kCustom, calls=%fused_computation.1 | custom fusion | bytes 1049600 | tf_op jit(solution)/shard_map/gather | solution.py:480
  93.5 2.9 %fusion.14 = bf16[256,1,2,256]{0,3,2,1:T(8,128)(2,1)S(1)} fusion(bf16[2560,256]{1,0:T(8,128)(2,1)} %param.23, f32[256,1,2,256]{0,3,2,1:T(8,128)} %bitcast.133, f32[1,2,256,256]{2,3,1,0:T(8,128)} %copy-done.3, f32[2,256]{1,0:T(2,128)S(1)} %fusion.24, f32[256,2]{0,1:T(2,128)S(1)} %get-tuple-element.7, f32[256,2]{0,1:T(2,128)S(1)} %get-tuple-element.8, ...), kind=kOutput, calls=%fused_computation.21 | convolution fusion | flops 406257664 | bytes 3951616 | tf_op jit(solution)/shard_map/gqts,sgd->tgqd/dot_general | solution.py:37
  96.4 2.0 convolution_convert_fusion
  98.4 3.1 %convert_element_type.88 = f32[256,2560]{1,0:T(8,128)} convert(bf16[256,2560]{1,0:T(8,128)(2,1)} %param.19) | non-fusion elementwise | flops 655360 | bytes 3932160 | tf_op jit(solution)/shard_map/convert_element_type | solution.py:425
  102.1 43.1 %all-reduce.2.cloned.1.call-done = bf16[256,2560]{1,0:T(8,128)(2,1)} async-done(((bf16[256,2560]{1,0:T(8,128)(2,1)}), bf16[256,2560]{1,0:T(8,128)(2,1)}) %all-reduce.2.cloned.1.call-update) | async-done | bytes 1310736 | tf_op jit(solution)/shard_map/psum | solution.py:494
  146.4 1.5 multiply_reduce_fusion.1
  148.9 68.9 %ffn_block.1 = bf16[64,2560]{1,0:T(8,128)(2,1)} custom-call(bf16[64,2560]{1,0:T(8,128)(2,1)} %multiply_convert_fusion.1.ffw_in_ref, f32[64,2560]{1,0:T(8,128)} %copy-done.2, f32[1,2560]{1,0:T(1,128)} %broadcast_in_dim.10.gain_ref, bf16[320,2560]{1,0:T(8,128)(2,1)} %bitcast.130, bf16[320,2560]{1,0:T(8,128)(2,1)} %bitcast.131, bf16[320,2560]{1,0:T(8,128)(2,1)} %down_ref.1), custom_call_target="tpu_custom_call" | custom-call | tf_op jit(solution)/shard_map/ffn_block/pallas_call | solution.py:363
  217.8 1.7 copy.134
  (69 shorter events, 11.4 us)
Async XLA Ops:
  6.5 89.8 %copy-start = (bf16[512,2560]{1,0:T(8,128)(2,1)S(1)}, bf16[512,2560]{1,0:T(8,128)(2,1)}, u32[]{:S(2)}) copy-start(bf16[512,2560]{1,0:T(8,128)(2,1)} %param.26) | copy-start | bytes 7864324
  12.4 2.2 copy-start.9
  12.4 2.2 copy-start.10
  12.4 2.2 copy-start.11
  14.6 10.6 %copy-start.8 = (s32[256]{0:T(256)S(1)}, s32[256]{0:T(256)}, u32[]{:S(2)}) copy-start(s32[256]{0:T(256)} %param.35) | copy-start | bytes 3076
  14.6 10.7 %copy-start.13 = (f32[2560]{0:T(1024)S(1)}, f32[2560]{0:T(1024)}, u32[]{:S(2)}) copy-start(f32[2560]{0:T(1024)} %param.20) | copy-start | bytes 30724
  17.6 24.9 %all-to-all-start = ((bf16[32,32,512]{2,1,0:T(8,128)(2,1)}), bf16[32,32,512]{2,1,0:T(8,128)(2,1)}, u32[]{:S(2)}, u32[]{:S(2)}) async-start(bf16[32,32,512]{2,1,0:T(8,128)(2,1)} %bitcast.127), calls=%async_computation | async-start | bytes 2097152 | tf_op jit(solution)/shard_map/all_to_all | solution.py:469
  25.3 19.4 %copy-start.4 = (bf16[1,512,256]{2,1,0:T(8,128)(2,1)S(1)}, bf16[1,512,256]{2,1,0:T(8,128)(2,1)}, u32[]{:S(2)}) copy-start(bf16[1,512,256]{2,1,0:T(8,128)(2,1)} %param.33) | copy-start | bytes 786436
  46.7 1.9 copy-start.1
  46.7 7.1 %copy-start.12 = (bf16[1,512,256]{2,1,0:T(8,128)(2,1)S(1)}, bf16[1,512,256]{2,1,0:T(8,128)(2,1)}, u32[]{:S(2)}) copy-start(bf16[1,512,256]{2,1,0:T(8,128)(2,1)} %param.34) | copy-start | bytes 786436
  50.0 12.0 %all-to-all-start.1 = ((bf16[32,32,2]{1,2,0:T(2,128)(2,1)}), bf16[32,32,2]{1,2,0:T(2,128)(2,1)S(1)}, u32[]{:S(2)}, u32[]{:S(2)}) async-start(bf16[32,32,2]{1,2,0:T(2,128)(2,1)} %copy.99), calls=%async_computation.1 | async-start | bytes 32768 | tf_op jit(solution)/shard_map/all_to_all | solution.py:477
  59.4 10.3 %copy-start.15 = (f32[256]{0:T(256)S(1)}, f32[256]{0:T(256)}, u32[]{:S(2)}) copy-start(f32[256]{0:T(256)} %param.25) | copy-start | bytes 3076
  59.4 10.3 %copy-start.16 = (f32[256,256]{0,1:T(8,128)S(1)}, f32[256,256]{0,1:T(8,128)}, u32[]{:S(2)}) copy-start(f32[256,256]{0,1:T(8,128)} %get-tuple-element.14) | copy-start | bytes 786436
  62.0 24.8 %all-to-all-start.2 = ((bf16[32,32,512]{2,1,0:T(8,128)(2,1)}), bf16[32,32,512]{2,1,0:T(8,128)(2,1)}, u32[]{:S(2)}, u32[]{:S(2)}) async-start(bf16[32,32,512]{2,1,0:T(8,128)(2,1)} %convert_element_type.102), calls=%async_computation.2 | async-start | bytes 2097152 | tf_op jit(solution)/shard_map/all_to_all | solution.py:474
  69.5 75.8 %all-reduce.2.cloned.1.call-start = ((), (), s32[]{:S(2)}) async-start(), calls=%async_computation.3 | async-start | bytes 2621440 | tf_op jit(solution)/shard_map/psum | solution.py:494
  70.1 0.8 copy-start.3
  89.7 3.8 %copy-start.14 = (f32[2560]{0:T(1024)S(1)}, f32[2560]{0:T(1024)}, u32[]{:S(2)}) copy-start(f32[2560]{0:T(1024)} %param.20) | copy-start | bytes 30724
  98.3 3.2 %copy-start.7 = (f32[2560]{0:T(1024)S(1)}, f32[2560]{0:T(1024)}, u32[]{:S(2)}) copy-start(f32[2560]{0:T(1024)} %param.32) | copy-start | bytes 30724
  98.3 48.1 %copy-start.5 = (f32[2560]{0:T(1024)S(1)}, f32[2560]{0:T(1024)}, u32[]{:S(2)}) copy-start(f32[2560]{0:T(1024)} %param.27) | copy-start | bytes 30724
  98.4 49.6 %copy-start.6 = (f32[2560]{0:T(1024)S(1)}, f32[2560]{0:T(1024)}, u32[]{:S(2)}) copy-start(f32[2560]{0:T(1024)} %param.28) | copy-start | bytes 30724
  147.9 1.0 copy-start.2
Sparse Core Ops, SparseCore 0:
  98.5 46.7 all-reduce.1

commit v2 on v1

--- a/solution.py
+++ b/solution.py
@@ -16,49 +16,6 @@
         values_in
         * lax.rsqrt(jnp.mean(values_in * values_in, axis=-1, keepdims=True) + EPS)
         * gain_vec
-    )
-
-
-def local_attention(query_rows, key_rows, value_rows, segment_rows, score_scale):
-    scores = (
-        jnp.einsum("tgqd,sgd->gqts", query_rows, key_rows, preferred_element_type=jnp.float32)
-        * score_scale
-    )
-    row_count = segment_rows.shape[0]
-    token_position = jnp.arange(row_count, dtype=jnp.int32)
-    allowed = (segment_rows[:, None] == segment_rows[None, :]) & (
-        token_position[:, None] >= token_position[None, :]
-    )
-    scores = jnp.where(allowed, scores, -jnp.inf)
-    row_max = jnp.max(scores, axis=-1, keepdims=True)
-    powers = jnp.exp(scores - row_max)
-    row_sum = jnp.sum(powers, axis=-1, keepdims=True)
-    weights = (powers / row_sum).astype(jnp.bfloat16)
-    mixed = jnp.einsum("gqts,sgd->tgqd", weights, value_rows, preferred_element_type=jnp.float32)
-    log_total = jnp.transpose((row_max + jnp.log(row_sum))[..., 0], (2, 0, 1))
-    return (mixed, log_total)
-
-
-def prefix_partials(incoming, stored_keys, stored_values, score_scale):
-    sources, slot_count, head_cols = incoming.shape
-    kv_heads = stored_keys.shape[1]
-    head_dim = stored_keys.shape[2]
-    query_group_width = head_cols // (kv_heads * head_dim)
-    query_rows = incoming.reshape(sources * slot_count, kv_heads, query_group_width, head_dim)
-    scores = (
-        jnp.einsum("rgqd,kgd->rgqk", query_rows, stored_keys, preferred_element_type=jnp.float32)
-        * score_scale
-    )
-    row_max = jnp.max(scores, axis=-1, keepdims=True)
-    powers = jnp.exp(scores - row_max)
-    row_sum = jnp.sum(powers, axis=-1, keepdims=True)
-    weights = (powers / row_sum).astype(jnp.bfloat16)
-    mixed = jnp.einsum("rgqk,kgd->rgqd", weights, stored_values, preferred_element_type=jnp.float32)
-    mixed = lax.optimization_barrier(mixed.astype(jnp.bfloat16)).astype(jnp.float32)
-    log_total = row_max[..., 0] + jnp.log(row_sum[..., 0])
-    return (
-        mixed.reshape(sources, slot_count, head_cols),
-        log_total.reshape(sources, slot_count, kv_heads * query_group_width),
     )
 
 
@@ -391,6 +348,265 @@
     )(ffw_in, residual, gain, gate_t, up_t, down_weight)
 
 
+def plane_place():
+    me = lax.axis_index("req")
+    layer = lax.axis_index("mlp")
+    core = lax.rem(me, 2)
+    chip = me // 2
+    return chip // RING, lax.rem(chip, RING), core, layer
+
+
+def attention_kernel(
+    states_ref,
+    attn_gain_ref,
+    query_gain_ref,
+    key_gain_ref,
+    segment_ref,
+    prefix_ref,
+    owner_ref,
+    query_w_ref,
+    key_w_ref,
+    value_w_ref,
+    keys_ref,
+    values_ref,
+    out_ref,
+    query_w,
+    key_w,
+    value_w,
+    stored_keys,
+    stored_values,
+    outgoing,
+    incoming,
+    results,
+    back,
+    local_sem,
+    send_sem,
+    recv_sem,
+    back_send_sem,
+    back_recv_sem,
+):
+    row, col, core, layer = plane_place()
+    rows, width = states_ref.shape
+    head = query_gain_ref.shape[1]
+    heads = query_w.shape[1] // head
+    peers = 2 * RING * RING
+    score_scale = head ** (-0.5)
+    f32, bf16 = jnp.float32, jnp.bfloat16
+
+    def shifted(offset, sign):
+        down, across, flip = offset // (2 * RING), (offset // 2) % RING, offset % 2
+        if sign < 0:
+            down, across = (RING - down) % RING, (RING - across) % RING
+        row_at = lax.rem(row + down, RING)
+        col_at = lax.rem(col + across, RING)
+        core_at = 1 - core if flip else core
+        return ((row_at * RING + col_at) * 2 + core_at, layer)
+
+    barrier = pltpu.get_barrier_semaphore()
+    for offset in range(1, peers):
+        pl.semaphore_signal(barrier, inc=1, device_id=shifted(offset, 1), device_id_type=MESH_ID)
+    local = []
+    for index, (src, dst) in enumerate(
+        (
+            (query_w_ref, query_w),
+            (key_w_ref, key_w),
+            (value_w_ref, value_w),
+            (keys_ref, stored_keys),
+            (values_ref, stored_values),
+        )
+    ):
+        copy = pltpu.make_async_copy(src, dst, local_sem.at[index])
+        copy.start()
+        local.append(copy)
+
+    normalized = normed(states_ref[...].astype(f32), attn_gain_ref[...]).astype(bf16)
+
+    def column(line):
+        return jnp.transpose(jnp.broadcast_to(line, (128, rows)))[:, :1]
+
+    prefix_row = prefix_ref[...].astype(f32)
+    prefix_col = column(prefix_row)
+    row_at = lax.broadcasted_iota(jnp.int32, (rows, rows), 0)
+    col_at = lax.broadcasted_iota(jnp.int32, (rows, rows), 1)
+    same = jnp.where(prefix_col == prefix_row, 1.0, 0.0)
+    rank_col = jnp.sum(jnp.where(col_at < row_at, same, 0.0), axis=1, keepdims=True)
+    rank_row = jnp.sum(jnp.where(row_at < col_at, same, 0.0), axis=0, keepdims=True)
+    groups = owner_ref.shape[1]
+    onehot = prefix_col == lax.broadcasted_iota(jnp.int32, (rows, groups), 1).astype(f32)
+    owner_col = jnp.sum(jnp.where(onehot, owner_ref[...].astype(f32), 0.0), axis=1, keepdims=True)
+    owner_row = jnp.transpose(jnp.broadcast_to(owner_col, (rows, 128)))[:1]
+
+    def place(owner, rank):
+        owner = owner.astype(jnp.int32)
+        down = ((owner >> 3) - row) & 3
+        across = (((owner >> 1) & 3) - col) & 3
+        flip = ((owner & 1) - core) & 1
+        return (down * 8 + across * 2 + flip) * CAP + rank.astype(jnp.int32)
+
+    place_col = place(owner_col, rank_col)
+    place_row = place(owner_row, rank_row)
+
+    local[0].wait()
+    raw = jnp.dot(normalized, query_w[...], preferred_element_type=f32)
+    queries = [
+        normed(raw[:, g * head : (g + 1) * head], query_gain_ref[...]).astype(bf16)
+        for g in range(heads)
+    ]
+    query_rows = jnp.concatenate(queries, axis=1)
+    pl.semaphore_wait(barrier, peers - 1)
+    sends = {}
+    batch = 2 * RING
+    for part in range(peers // batch):
+        slots = lax.broadcasted_iota(jnp.int32, (batch * CAP, rows), 0) + part * batch * CAP
+        placing = jnp.where(slots == place_row, 1.0, 0.0).astype(bf16)
+        packed = jnp.dot(placing, query_rows, preferred_element_type=f32).astype(bf16)
+        packed = packed.reshape(batch, CAP, heads * head)
+        if part == 0:
+            incoming[0] = packed[0]
+        outgoing[pl.ds(part * batch, batch)] = packed
+        for offset in range(max(part * batch, 1), (part + 1) * batch):
+            copy = pltpu.make_async_remote_copy(
+                src_ref=outgoing.at[offset],
+                dst_ref=incoming.at[offset],
+                send_sem=send_sem.at[offset],
+                recv_sem=recv_sem.at[offset],
+                device_id=shifted(offset, 1),
+                device_id_type=MESH_ID,
+            )
+            copy.start()
+            sends[offset] = copy
+
+    local[1].wait()
+    local[2].wait()
+    raw = jnp.dot(normalized, key_w[...], preferred_element_type=f32)
+    keys = normed(raw, key_gain_ref[...]).astype(bf16)
+    values = jnp.dot(normalized, value_w[...], preferred_element_type=f32).astype(bf16)
+    segment_row = segment_ref[...].astype(f32)
+    allowed = (column(segment_row) == segment_row) & (row_at >= col_at)
+
+    def attend(query, key, value, mask):
+        scores = (
+            lax.dot_general(query, key, (((1,), (1,)), ((), ())), preferred_element_type=f32)
+            * score_scale
+        )
+        if mask is not None:
+            scores = jnp.where(mask, scores, -jnp.inf)
+        row_max = jnp.max(scores, axis=-1, keepdims=True)
+        powers = jnp.exp(scores - row_max)
+        total = jnp.sum(powers, axis=-1, keepdims=True)
+        weights = (powers / total).astype(bf16)
+        mixed = jnp.dot(weights, value, preferred_element_type=f32)
+        return mixed, row_max + jnp.log(total)
+
+    suffix = [attend(query, keys, values, allowed) for query in queries]
+
+    local[3].wait()
+    local[4].wait()
+    lanes = lax.broadcasted_iota(jnp.int32, (batch * CAP, 128), 1)
+    returns = {}
+    for part in range(peers // batch):
+        for offset in range(max(part * batch, 1), (part + 1) * batch):
+            sends[offset].wait_recv()
+        query = incoming[pl.ds(part * batch, batch)].reshape(batch * CAP, heads * head)
+        tail = jnp.zeros((batch * CAP, 128), f32)
+        for g in range(heads):
+            mixed, log_total = attend(
+                query[:, g * head : (g + 1) * head], stored_keys[...], stored_values[...], None
+            )
+            coarse = log_total.astype(bf16).astype(f32)
+            tail = jnp.where(lanes == 2 * g, coarse, tail)
+            tail = jnp.where(lanes == 2 * g + 1, log_total - coarse, tail)
+            results[pl.ds(part * batch, batch), :, pl.ds(g * head, head)] = mixed.astype(
+                bf16
+            ).reshape(batch, CAP, head)
+        results[pl.ds(part * batch, batch), :, pl.ds(heads * head, 128)] = tail.astype(
+            bf16
+        ).reshape(batch, CAP, 128)
+        if part == 0:
+            back[0] = results[0]
+        for offset in range(max(part * batch, 1), (part + 1) * batch):
+            copy = pltpu.make_async_remote_copy(
+                src_ref=results.at[offset],
+                dst_ref=back.at[offset],
+                send_sem=back_send_sem.at[offset],
+                recv_sem=back_recv_sem.at[offset],
+                device_id=shifted(offset, -1),
+                device_id_type=MESH_ID,
+            )
+            copy.start()
+            returns[offset] = copy
+
+    picked = jnp.zeros((rows, heads * head + 128), f32)
+    for part in range(peers // batch):
+        for offset in range(max(part * batch, 1), (part + 1) * batch):
+            returns[offset].wait_recv()
+        slots = lax.broadcasted_iota(jnp.int32, (rows, batch * CAP), 1) + part * batch * CAP
+        choosing = jnp.where(slots == place_col, 1.0, 0.0).astype(bf16)
+        block = back[pl.ds(part * batch, batch)].reshape(batch * CAP, heads * head + 128)
+        picked = picked + jnp.dot(choosing, block, preferred_element_type=f32)
+    for g in range(heads):
+        mixed, log_total = suffix[g]
+        at = heads * head + 2 * g
+        prefix_lse = picked[:, at : at + 1] + picked[:, at + 1 : at + 2]
+        blend = jax.nn.sigmoid(prefix_lse - log_total)
+        columns = slice(g * head, (g + 1) * head)
+        out_ref[:, columns] = (blend * picked[:, columns] + (1.0 - blend) * mixed).astype(bf16)
+
+    for offset in range(1, peers):
+        sends[offset].wait_send()
+        returns[offset].wait_send()
+
+
+def attention_block(
+    states, attn_gain, query_gain, key_gain, segment, prefix_id, owner_map, query_w, key_w, value_w, keys, values
+):
+    rows, width = states.shape
+    vmem = pl.BlockSpec(memory_space=pltpu.VMEM)
+    hbm = pl.BlockSpec(memory_space=pl.ANY)
+    bf16 = jnp.bfloat16
+    peers = 2 * RING * RING
+    cols = query_w.shape[1]
+    return pl.pallas_call(
+        attention_kernel,
+        out_shape=jax.ShapeDtypeStruct((rows, cols), bf16),
+        in_specs=[vmem] * 7 + [hbm] * 5,
+        out_specs=vmem,
+        scratch_shapes=[
+            pltpu.VMEM(query_w.shape, bf16),
+            pltpu.VMEM(key_w.shape, bf16),
+            pltpu.VMEM(value_w.shape, bf16),
+            pltpu.VMEM(keys.shape, bf16),
+            pltpu.VMEM(values.shape, bf16),
+            pltpu.VMEM((peers, CAP, cols), bf16),
+            pltpu.VMEM((peers, CAP, cols), bf16),
+            pltpu.VMEM((peers, CAP, cols + 128), bf16),
+            pltpu.VMEM((peers, CAP, cols + 128), bf16),
+            pltpu.SemaphoreType.DMA((5,)),
+            pltpu.SemaphoreType.DMA((peers,)),
+            pltpu.SemaphoreType.DMA((peers,)),
+            pltpu.SemaphoreType.DMA((peers,)),
+            pltpu.SemaphoreType.DMA((peers,)),
+        ],
+        compiler_params=pltpu.CompilerParams(
+            collective_id=1, has_side_effects=True, vmem_limit_bytes=58 << 20
+        ),
+        name="attention_block",
+    )(
+        states,
+        attn_gain,
+        query_gain,
+        key_gain,
+        segment,
+        prefix_id,
+        owner_map,
+        query_w,
+        key_w,
+        value_w,
+        keys,
+        values,
+    )
+
+
 def body(
     states,
     attn_gain,
@@ -412,83 +628,23 @@
     prefix_id,
     owner_map,
 ):
-    row_count = states.shape[0]
-    head_dim = query_gain.shape[0]
-    kv_heads = key_matrix.shape[1] // head_dim
-    head_cols = query_matrix.shape[1]
-    query_group_width = head_cols // (kv_heads * head_dim)
-    score_scale = head_dim ** (-0.5)
-    req_count = lax.axis_size("req")
     mlp_count = lax.axis_size("mlp")
     mlp_index = lax.axis_index("mlp")
-    quarter = row_count // mlp_count
+    quarter = states.shape[0] // mlp_count
     states_f = states.astype(jnp.float32)
-    normalized_input = normed(states_f, attn_gain).astype(jnp.bfloat16)
-    unnormed_queries = jnp.dot(
-        normalized_input, query_matrix, preferred_element_type=jnp.float32
-    ).reshape(row_count, kv_heads, query_group_width, head_dim)
-    query_vectors = normed(unnormed_queries, query_gain).astype(jnp.bfloat16)
-    unnormed_keys = jnp.dot(
-        normalized_input, key_matrix, preferred_element_type=jnp.float32
-    ).reshape(row_count, kv_heads, head_dim)
-    key_vectors = normed(unnormed_keys, key_gain).astype(jnp.bfloat16)
-    value_vectors = (
-        jnp.dot(normalized_input, value_matrix, preferred_element_type=jnp.float32)
-        .astype(jnp.bfloat16)
-        .reshape(row_count, kv_heads, head_dim)
-    )
-    prefix_count = owner_map.shape[0]
-    prefix_onehot = (
-        prefix_id[:, None] == jnp.arange(prefix_count, dtype=jnp.int32)[None, :]
-    ).astype(jnp.int32)
-    target = jnp.sum(prefix_onehot * owner_map[None, :], axis=1)
-    to_owner = (target[:, None] == jnp.arange(req_count, dtype=jnp.int32)[None, :]).astype(
-        jnp.float32
-    )
-    token_position = jnp.arange(row_count, dtype=jnp.int32)
-    earlier = (token_position[:, None] > token_position[None, :]).astype(jnp.float32)
-    counts = jnp.dot(earlier, to_owner, precision=lax.Precision.HIGHEST)
-    slot_index = jnp.sum(to_owner * counts, axis=1).astype(jnp.int32)
-    place_row = target * CAP + slot_index
-    placing = (place_row[None, :] == jnp.arange(req_count * CAP, dtype=jnp.int32)[:, None]).astype(
-        jnp.bfloat16
-    )
-    outgoing = (
-        jnp.dot(
-            placing, query_vectors.reshape(row_count, head_cols), preferred_element_type=jnp.float32
-        )
-        .astype(jnp.bfloat16)
-        .reshape(req_count, CAP, head_cols)
-    )
-    stored_keys = prefix_key_cache[0].reshape(-1, kv_heads, head_dim)
-    stored_values = prefix_value_cache[0].reshape(-1, kv_heads, head_dim)
-    suffix_output, suffix_log_sum = local_attention(
-        query_vectors, key_vectors, value_vectors, segment, score_scale
-    )
-    mixed, log_total = prefix_partials(
-        lax.all_to_all(outgoing, "req", split_axis=0, concat_axis=0, tiled=True),
-        stored_keys,
-        stored_values,
-        score_scale,
-    )
-    back_out = lax.all_to_all(
-        mixed.astype(jnp.bfloat16), "req", split_axis=0, concat_axis=0, tiled=True
-    ).astype(mixed.dtype)
-    back_lse = lax.all_to_all(
-        log_total.astype(jnp.bfloat16), "req", split_axis=0, concat_axis=0, tiled=True
-    ).astype(log_total.dtype)
-    prefix_out = back_out.reshape(req_count * CAP, head_cols)[place_row].reshape(
-        row_count, kv_heads, query_group_width, head_dim
-    )
-    prefix_lse = back_lse.reshape(req_count * CAP, kv_heads * query_group_width)[place_row].reshape(
-        row_count, kv_heads, query_group_width
-    )
-    prefix_out, prefix_lse = (prefix_out, prefix_lse)
-    blend = jax.nn.sigmoid(prefix_lse - suffix_log_sum)[..., None]
-    attended = (
-        (blend * prefix_out + (1.0 - blend) * suffix_output)
-        .astype(jnp.bfloat16)
-        .reshape(row_count, head_cols)
+    attended = attention_block(
+        states,
+        attn_gain[None],
+        query_gain[None],
+        key_gain[None],
+        segment[None],
+        prefix_id[None],
+        owner_map[None],
+        query_matrix,
+        key_matrix,
+        value_matrix,
+        prefix_key_cache[0],
+        prefix_value_cache[0],
     )
     partial_value = jnp.dot(attended, out_weight, preferred_element_type=jnp.float32)
     full_sum = lax.psum(partial_value.astype(jnp.bfloat16), "mlp").astype(jnp.float32)

time: 228 us -> 185 us (0.81)
  Pallas kernels: 68.9 us -> 113 us
  waiting for transfers between devices: 71.8 us -> 47 us
  starting transfers between devices: 19 us -> 0.01 us
  matrix products: 19.7 us -> 2.88 us
  local copies, waits for them, and re-layouts: 19.2 us -> 3.81 us
  other arithmetic: 14 us -> 3.46 us
    pallas_call x0 -> x1, Pallas kernels: none -> 43.1 us  [attention_block(): pl.pallas_call(attention_kernel, out_shape=jax.ShapeDtypeStruct((rows, co...]
    all_to_all x3 -> x0, waiting for transfers between devices: 28.7 us -> none  [the longest x1 14.8 us: body(): lax.all_to_all(mixed.astype(jnp.bfloat16), 'req', split_axis=0, concat_ax...]
    all_to_all x3 -> x0, starting transfers between devices: 18.8 us -> none  [the longest x1 7.53 us: body(): lax.all_to_all(outgoing, 'req', split_axis=0, concat_axis=0, tiled=True)]
    dot_general x8 -> x0, matrix products: 17.7 us -> none  [the longest x1 4.06 us: body(): jnp.dot(normalized_input, query_matrix, preferred_element_type=jnp.float32)]
    gather x4 -> x0, local copies, waits for them, and re-layouts: 4.6 us -> none  [the longest x2 3.8 us: body(): back_out.reshape(req_count * CAP, head_cols)[place_row]]
    convert_element_type x3 -> x0, other arithmetic: 4.3 us -> none  [the longest x1 3.13 us: body(): states_f = states.astype(jnp.float32)]
    psum x1, waiting for transfers between devices: 43.1 us -> 47 us  [body(): lax.psum(partial_value.astype(jnp.bfloat16), 'mlp').astype(jnp.float32)]
    convert_element_type x3 -> x0, local copies, waits for them, and re-layouts: 3.27 us -> none  [the longest x1 2.57 us: body(): mixed.astype(jnp.bfloat16)]
  transfers between devices with their start and end apart: 4 -> 1, of which waited for: 3 -> 1; matrix products, arithmetic and copies ran while one was open for 7% -> 0% of each run, Pallas kernels for 0% -> 0%
where the time goes in v2:
time: 185 us; the launch traced here: 183 us
  Pallas kernels  113 us (61%)
  waiting for transfers between devices  47 us (25%)
  between operations  13.5 us (7%)
  local copies, waits for them, and re-layouts  3.81 us (2%)
  other arithmetic  3.46 us (2%)
  matrix products  2.88 us (2%)
    pallas_call x1, Pallas kernels, ffn_block(): pl.pallas_call(ffn_kernel, out_shape=jax.ShapeDtypeStruct((rows, width),...  69.4 us
    psum x1, waiting for transfers between devices, body(): lax.psum(partial_value.astype(jnp.bfloat16), 'mlp').astype(jnp.float32)  47 us
    pallas_call x1, Pallas kernels, attention_block(): pl.pallas_call(attention_kernel, out_shape=jax.ShapeDtypeStruct((rows, co...  43.1 us
  transfers between devices with their start and end apart: 1, of which 1 were waited for; matrix products, arithmetic and copies ran while one was open for 0% of the time, Pallas kernels for 0%

profile of v2, /device:TPU:0, one launch (start us, length us, event | category | flops | bytes accessed | tf_op | source)
XLA Modules:
  0.0 183.2 jit_solution(13432766626408210018)
XLA Ops:
  6.5 0.0 copy-start
  6.5 0.0 all-reduce.2.cloned.1.call-start
  6.5 1.5 broadcast_in_dim.25.attn_gain_ref
  8.0 43.1 %attention_block.1 = bf16[256,512]{1,0:T(8,128)(2,1)} custom-call(bf16[256,2560]{1,0:T(8,128)(2,1)} %states_ref.1, f32[1,2560]{1,0:T(1,128)} %broadcast_in_dim.25.attn_gain_ref, f32[1,256]{1,0:T(1,128)} %bitcast.15, f32[1,256]{1,0:T(1,128)} %bitcast.16, s32[1,256]{1,0:T(1,128)} %bitcast.17, s32[1,256]{1,0:T(1,128)} %bitcast.18, s32[1,32]{1,0:T(1,128)} %bitcast.19, ...), custom_call_target="tpu_custom_call" | custom-call | tf_op jit(solution)/shard_map/attention_block/pallas_call | solution.py:569
  51.1 0.0 copy-done
  51.1 0.0 copy-start.4
  51.2 2.9 %convolution_convert_fusion = bf16[256,2560]{1,0:T(8,128)(2,1)} fusion(bf16[256,512]{1,0:T(8,128)(2,1)} %attention_block.1, bf16[512,2560]{1,0:T(8,128)(2,1)S(1)} %copy-done), kind=kOutput, calls=%fused_computation | convolution fusion | flops 671744000 | bytes 4194304 | tf_op jit(solution)/shard_map/dot_general | solution.py:649
  54.0 0.0 copy-start.2
  54.0 0.0 copy-start.3
  54.0 0.0 all-reduce.2.cloned.1.call-update
  54.1 0.0 copy-done.4
  54.1 0.6 broadcast_in_dim.31.gain_ref
  54.7 47.0 %all-reduce.2.cloned.1.call-done = bf16[256,2560]{1,0:T(8,128)(2,1)} async-done(((bf16[256,2560]{1,0:T(8,128)(2,1)}), bf16[256,2560]{1,0:T(8,128)(2,1)}) %all-reduce.2.cloned.1.call-update) | async-done | bytes 1310736 | tf_op jit(solution)/shard_map/psum | solution.py:650
  101.7 1.1 fusion.2
  102.9 0.0 copy-done.2
  102.9 1.4 multiply_reduce_fusion
  104.3 0.0 copy-start.1
  104.3 0.0 copy-done.3
  104.3 0.9 multiply_convert_fusion.ffw_in_ref
  105.2 0.0 copy-done.1
  105.2 69.4 %ffn_block.1 = bf16[64,2560]{1,0:T(8,128)(2,1)} custom-call(bf16[64,2560]{1,0:T(8,128)(2,1)} %multiply_convert_fusion.ffw_in_ref, f32[64,2560]{1,0:T(8,128)} %copy-done.1, f32[1,2560]{1,0:T(1,128)} %broadcast_in_dim.31.gain_ref, bf16[320,2560]{1,0:T(8,128)(2,1)} %bitcast.11, bf16[320,2560]{1,0:T(8,128)(2,1)} %bitcast.12, bf16[320,2560]{1,0:T(8,128)(2,1)} %down_ref.1), custom_call_target="tpu_custom_call" | custom-call | tf_op jit(solution)/shard_map/ffn_block/pallas_call | solution.py:320
  174.6 1.7 copy.22
  (2 shorter events, 0.0 us)
Async XLA Ops:
  6.5 44.6 %copy-start = (bf16[512,2560]{1,0:T(8,128)(2,1)S(1)}, bf16[512,2560]{1,0:T(8,128)(2,1)}, u32[]{:S(2)}) copy-start(bf16[512,2560]{1,0:T(8,128)(2,1)} %param.26) | copy-start | bytes 7864324
  6.5 95.2 %all-reduce.2.cloned.1.call-start = ((), (), s32[]{:S(2)}) async-start(), calls=%async_computation | async-start | bytes 2621440 | tf_op jit(solution)/shard_map/psum | solution.py:650
  51.1 2.9 %copy-start.4 = (f32[2560]{0:T(1024)S(1)}, f32[2560]{0:T(1024)}, u32[]{:S(2)}) copy-start(f32[2560]{0:T(1024)} %param.32) | copy-start | bytes 30724
  54.0 48.8 %copy-start.2 = (f32[2560]{0:T(1024)S(1)}, f32[2560]{0:T(1024)}, u32[]{:S(2)}) copy-start(f32[2560]{0:T(1024)} %param.27) | copy-start | bytes 30724
  54.0 50.3 %copy-start.3 = (f32[2560]{0:T(1024)S(1)}, f32[2560]{0:T(1024)}, u32[]{:S(2)}) copy-start(f32[2560]{0:T(1024)} %param.28) | copy-start | bytes 30724
  104.3 1.0 copy-start.1
Sparse Core Ops, SparseCore 0:
  54.2 47.4 all-reduce.1

commit v3 on v2

--- a/solution.py
+++ b/solution.py
@@ -41,17 +41,29 @@
     right = at(row, lax.rem(col + 1, RING), core)
     left = at(row, lax.rem(col + RING - 1, RING), core)
     sibling = at(row, col, 1 - core)
-    return right, left, up, down, sibling
+    above = (me, lax.rem(layer + 1, RING))
+    below = (me, lax.rem(layer + RING - 1, RING))
+    return right, left, up, down, sibling, above, below
 
 
 def ffn_kernel(
-    ffw_in_ref,
-    residual_ref,
+    attended_ref,
+    post_gain_ref,
+    ffw_gain_ref,
     gain_ref,
+    states_ref,
+    out_w_ref,
     gate_ref,
     up_ref,
     down_ref,
     out_ref,
+    out_w,
+    own_states,
+    layer_out,
+    layer_opposite,
+    layer_merged,
+    layer_side,
+    residual,
     rows_buf,
     gate_up,
     down_w,
@@ -70,10 +82,14 @@
     weight_send,
     weight_recv,
 ):
-    right, left, upper, lower, sibling = torus_place()
+    right, left, upper, lower, sibling, above, below = torus_place()
+    layer = lax.axis_index("mlp")
+    quarter = 2 * SUB
+    f32, bf16 = jnp.float32, jnp.bfloat16
     hidden = gate_ref.shape[0]
     barrier = pltpu.get_barrier_semaphore()
-    for peer in (right, left, upper, lower, sibling):
+    neighbours = (right, left, upper, lower, sibling, above, below)
+    for peer in neighbours:
         pl.semaphore_signal(barrier, inc=1, device_id=peer, device_id_type=MESH_ID)
 
     first = ((right, left), (upper, lower))
@@ -96,6 +112,13 @@
         copies.append(copy)
         return copy
 
+    layer_copies = []
+    for index, (src, dst) in enumerate(
+        ((out_w_ref, out_w), (states_ref.at[pl.ds(layer * quarter, quarter)], own_states))
+    ):
+        copy = pltpu.make_async_copy(src, dst, local_sem.at[3 + index])
+        copy.start()
+        layer_copies.append(copy)
     local = []
     sources = (gate_ref, up_ref, down_ref)
     targets = (
@@ -116,40 +139,29 @@
     def slot(group, chunk, sub, start=0, size=SUB):
         return rows_buf.at[chunk, pl.ds(group * RING * SUB + sub * SUB + start, size)]
 
-    for group in range(2):
-        rows_buf[0, pl.ds(group * RING * SUB, SUB)] = ffw_in_ref[pl.ds(group * SUB, SUB)]
-    pl.semaphore_wait(barrier, 5)
-
-    step1 = []
-    for group in range(2):
-        plus, minus = first[group]
-        step1.append(
+    for copy in layer_copies:
+        copy.wait()
+
+    def projected(offset):
+        rows = pl.ds(lax.rem(layer + offset, RING) * quarter, quarter)
+        return jnp.dot(attended_ref[rows], out_w[...], preferred_element_type=f32)
+
+    layer_out[2] = projected(2).astype(bf16)
+    pl.semaphore_wait(barrier, len(neighbours))
+    layer_opp = []
+    for group in range(2):
+        layer_opp.append(
             (
-                send(slot(group, 0, 0), slot(group, 0, 3), plus),
-                send(slot(group, 0, 0), slot(group, 0, 1), minus),
+                send(
+                    layer_out.at[2, pl.ds(group * SUB, HALF)], layer_opposite.at[0, group], above
+                ),
+                send(
+                    layer_out.at[2, pl.ds(group * SUB + HALF, HALF)],
+                    layer_opposite.at[1, group],
+                    below,
+                ),
             )
         )
-    across = {}
-
-    def send_across(group, sub):
-        plus, minus = second[group]
-        across[group, sub] = (
-            send(slot(group, 0, sub), slot(group, 3, sub), plus),
-            send(slot(group, 0, sub), slot(group, 1, sub), minus),
-        )
-
-    relays = {}
-
-    def relay_across(group, sub):
-        plus, minus = second[group]
-        across[group, sub][0].wait_recv()
-        a = send(slot(group, 3, sub, 0, HALF), slot(group, 2, sub, 0, HALF), plus)
-        across[group, sub][1].wait_recv()
-        b = send(slot(group, 1, sub, HALF, HALF), slot(group, 2, sub, HALF, HALF), minus)
-        relays[group, sub] = (a, b)
-
-    for group in range(2):
-        send_across(group, 0)
     weight_copies = []
     for index, (src, dst) in enumerate(zip(sources, far_targets)):
         copy = pltpu.make_async_remote_copy(
@@ -162,6 +174,91 @@
         )
         copy.start()
         weight_copies.append(copy)
+    layer_plain = []
+    nexts = projected(1)
+    layer_out[1] = nexts.astype(bf16)
+    for group in range(2):
+        layer_plain.append(
+            [
+                send(
+                    layer_out.at[1, pl.ds(group * SUB + HALF, HALF)],
+                    layer_side.at[0, group, pl.ds(HALF, HALF)],
+                    above,
+                )
+            ]
+        )
+    prevs = projected(3)
+    layer_out[3] = prevs.astype(bf16)
+    for group in range(2):
+        layer_plain[group].append(
+            send(
+                layer_out.at[3, pl.ds(group * SUB, HALF)],
+                layer_side.at[1, group, pl.ds(0, HALF)],
+                below,
+            )
+        )
+    layer_far = []
+    for group in range(2):
+        start = group * SUB
+        layer_opp[group][0].wait_recv()
+        layer_merged[0, group] = (
+            layer_out[1, pl.ds(start, HALF)].astype(f32) + layer_opposite[0, group].astype(f32)
+        ).astype(bf16)
+        a = send(layer_merged.at[0, group], layer_side.at[0, group, pl.ds(0, HALF)], above)
+        layer_opp[group][1].wait_recv()
+        layer_merged[1, group] = (
+            layer_out[3, pl.ds(start + HALF, HALF)].astype(f32)
+            + layer_opposite[1, group].astype(f32)
+        ).astype(bf16)
+        b = send(layer_merged.at[1, group], layer_side.at[1, group, pl.ds(HALF, HALF)], below)
+        layer_far.append((a, b))
+    residual[...] = projected(0)
+
+    def enter(group):
+        for copy in layer_plain[group]:
+            copy.wait_recv()
+        for copy in layer_far[group]:
+            copy.wait_recv()
+        rows = pl.ds(group * SUB, SUB)
+        total = (
+            residual[rows]
+            + layer_side[0, group].astype(f32)
+            + layer_side[1, group].astype(f32)
+        )
+        after = own_states[rows].astype(f32) + normed(total, post_gain_ref[...])
+        residual[rows] = after
+        rows_buf[0, pl.ds(group * RING * SUB, SUB)] = normed(after, ffw_gain_ref[...]).astype(bf16)
+
+    step1 = []
+    across = {}
+
+    def send_across(group, sub):
+        plus, minus = second[group]
+        across[group, sub] = (
+            send(slot(group, 0, sub), slot(group, 3, sub), plus),
+            send(slot(group, 0, sub), slot(group, 1, sub), minus),
+        )
+
+    relays = {}
+
+    def relay_across(group, sub):
+        plus, minus = second[group]
+        across[group, sub][0].wait_recv()
+        a = send(slot(group, 3, sub, 0, HALF), slot(group, 2, sub, 0, HALF), plus)
+        across[group, sub][1].wait_recv()
+        b = send(slot(group, 1, sub, HALF, HALF), slot(group, 2, sub, HALF, HALF), minus)
+        relays[group, sub] = (a, b)
+
+    for group in range(2):
+        plus, minus = first[group]
+        enter(group)
+        step1.append(
+            (
+                send(slot(group, 0, 0), slot(group, 0, 3), plus),
+                send(slot(group, 0, 0), slot(group, 0, 1), minus),
+            )
+        )
+        send_across(group, 0)
     step2 = []
     for group in range(2):
         plus, minus = first[group]
@@ -301,7 +398,7 @@
             last[group][index].wait_recv()
         total = own + side_in2[group, 0].astype(jnp.float32) + side_in2[group, 1].astype(jnp.float32)
         rows = pl.ds(group * SUB, SUB)
-        out_ref[rows] = (residual_ref[rows] + normed(total, gain_ref[...])).astype(out_ref.dtype)
+        out_ref[rows] = (residual[rows] + normed(total, gain_ref[...])).astype(out_ref.dtype)
 
     for copy in copies:
         copy.wait_send()
@@ -309,20 +406,30 @@
         copy.wait_send()
 
 
-def ffn_block(ffw_in, residual, gain, gate_t, up_t, down_weight):
-    rows, width = ffw_in.shape
+def ffn_block(
+    attended, post_gain, ffw_gain, gain, states, out_w, gate_t, up_t, down_weight
+):
+    width = states.shape[1]
+    rows = 2 * SUB
     hidden = gate_t.shape[0]
     vmem = pl.BlockSpec(memory_space=pltpu.VMEM)
     hbm = pl.BlockSpec(memory_space=pl.ANY)
     bf16 = jnp.bfloat16
     span = RING * SUB
-    copies = 64
+    copies = 76
     return pl.pallas_call(
         ffn_kernel,
         out_shape=jax.ShapeDtypeStruct((rows, width), bf16),
-        in_specs=[vmem, vmem, vmem, hbm, hbm, hbm],
+        in_specs=[vmem] * 4 + [hbm] * 5,
         out_specs=vmem,
         scratch_shapes=[
+            pltpu.VMEM(out_w.shape, bf16),
+            pltpu.VMEM((rows, width), bf16),
+            pltpu.VMEM((RING, rows, width), bf16),
+            pltpu.VMEM((2, 2, HALF, width), bf16),
+            pltpu.VMEM((2, 2, HALF, width), bf16),
+            pltpu.VMEM((2, 2, SUB, width), bf16),
+            pltpu.VMEM((rows, width), jnp.float32),
             pltpu.VMEM((RING, 2 * span, width), bf16),
             pltpu.VMEM((4 * hidden, width), bf16),
             pltpu.VMEM((2 * hidden, width), bf16),
@@ -335,7 +442,7 @@
             pltpu.VMEM((2, RING, SUB, width), bf16),
             pltpu.VMEM((2, 2, HALF, width), bf16),
             pltpu.VMEM((2, 2, SUB, width), bf16),
-            pltpu.SemaphoreType.DMA((3,)),
+            pltpu.SemaphoreType.DMA((5,)),
             pltpu.SemaphoreType.DMA((copies,)),
             pltpu.SemaphoreType.DMA((copies,)),
             pltpu.SemaphoreType.DMA((3,)),
@@ -345,7 +452,7 @@
             collective_id=0, has_side_effects=True, vmem_limit_bytes=58 << 20
         ),
         name="ffn_block",
-    )(ffw_in, residual, gain, gate_t, up_t, down_weight)
+    )(attended, post_gain, ffw_gain, gain, states, out_w, gate_t, up_t, down_weight)
 
 
 def plane_place():
@@ -628,10 +735,6 @@
     prefix_id,
     owner_map,
 ):
-    mlp_count = lax.axis_size("mlp")
-    mlp_index = lax.axis_index("mlp")
-    quarter = states.shape[0] // mlp_count
-    states_f = states.astype(jnp.float32)
     attended = attention_block(
         states,
         attn_gain[None],
@@ -646,14 +749,16 @@
         prefix_key_cache[0],
         prefix_value_cache[0],
     )
-    partial_value = jnp.dot(attended, out_weight, preferred_element_type=jnp.float32)
-    full_sum = lax.psum(partial_value.astype(jnp.bfloat16), "mlp").astype(jnp.float32)
-    summed = lax.dynamic_slice_in_dim(full_sum, mlp_index * quarter, quarter, 0)
-    own_rows = lax.dynamic_slice_in_dim(states_f, mlp_index * quarter, quarter, 0)
-    residual = own_rows + normed(summed, post_gain)
-    ffw_in = normed(residual, ffw_gain).astype(jnp.bfloat16)
     return ffn_block(
-        ffw_in, residual, post_ffw_gain[None], gate_weight.T, up_weight.T, down_weight
+        attended,
+        post_gain[None],
+        ffw_gain[None],
+        post_ffw_gain[None],
+        states,
+        out_weight,
+        gate_weight.T,
+        up_weight.T,
+        down_weight,
     )
 
 

time: 185 us -> 134 us (0.72)
  waiting for transfers between devices: 47 us -> 0 us
  Pallas kernels: 113 us -> 127 us
  between operations: 13.5 us -> 0.02 us
  other arithmetic: 3.46 us -> 0 us
  local copies, waits for them, and re-layouts: 3.81 us -> 6.95 us
  matrix products: 2.88 us -> 0 us
    psum x1 -> x0, waiting for transfers between devices: 47 us -> none  [body(): lax.psum(partial_value.astype(jnp.bfloat16), 'mlp').astype(jnp.float32)]
    pallas_call x1, Pallas kernels: 69.4 us -> 83.9 us  [ffn_block(): pl.pallas_call(ffn_kernel, out_shape=jax.ShapeDtypeStruct((rows, width),...]
    dot_general x1 -> x0, matrix products: 2.88 us -> none  [body(): jnp.dot(attended, out_weight, preferred_element_type=jnp.float32)]
    broadcast_in_dim x0 -> x2, local copies, waits for them, and re-layouts: none -> 2.62 us  [the longest x1 1.31 us: body(): post_gain[None]]
    reduce_sum x2 -> x0, other arithmetic: 2.53 us -> none  [normed(): jnp.mean(values_in * values_in, axis=-1, keepdims=True) + EPS]
  transfers between devices with their start and end apart: 1 -> 0, of which waited for: 1 -> 0; matrix products, arithmetic and copies ran while one was open for 0% -> 0% of each run, Pallas kernels for 0% -> 0%
where the time goes in v3:
time: 134 us
  Pallas kernels  127 us (95%)
  local copies, waits for them, and re-layouts  6.95 us (5%)
    pallas_call x1, Pallas kernels, ffn_block(): pl.pallas_call(ffn_kernel, out_shape=jax.ShapeDtypeStruct((rows, width),...  83.9 us
    pallas_call x1, Pallas kernels, attention_block(): pl.pallas_call(attention_kernel, out_shape=jax.ShapeDtypeStruct((rows, co...  43.1 us

profile of v3, /device:TPU:0, one launch (start us, length us, event | category | flops | bytes accessed | tf_op | source)
XLA Modules:
  0.0 134.0 jit_solution(6061159730658620206)
XLA Ops:
  0.0 1.3 broadcast_in_dim.27.attn_gain_ref
  1.3 1.3 broadcast_in_dim.33.post_gain_ref
  2.6 1.3 broadcast_in_dim.34.ffw_gain_ref
  3.9 1.3 broadcast_in_dim.35.gain_ref
  5.2 43.1 %attention_block.1.attended_ref = bf16[256,512]{1,0:T(8,128)(2,1)} custom-call(bf16[256,2560]{1,0:T(8,128)(2,1)} %states_ref.3, f32[1,2560]{1,0:T(1,128)} %broadcast_in_dim.27.attn_gain_ref, f32[1,256]{1,0:T(1,128)} %bitcast.13, f32[1,256]{1,0:T(1,128)} %bitcast.14, s32[1,256]{1,0:T(1,128)} %bitcast.15, s32[1,256]{1,0:T(1,128)} %bitcast.16, ...), custom_call_target="tpu_custom_call" | custom-call | tf_op jit(solution)/shard_map/attention_block/pallas_call | solution.py:676
  48.3 83.9 %ffn_block.1 = bf16[64,2560]{1,0:T(8,128)(2,1)} custom-call(bf16[256,512]{1,0:T(8,128)(2,1)} %attention_block.1.attended_ref, f32[1,2560]{1,0:T(1,128)} %broadcast_in_dim.33.post_gain_ref, f32[1,2560]{1,0:T(1,128)} %broadcast_in_dim.34.ffw_gain_ref, f32[1,2560]{1,0:T(1,128)} %broadcast_in_dim.35.gain_ref, bf16[256,2560]{1,0:T(8,128)(2,1)} %states_ref.3, ...), custom_call_target="tpu_custom_call" | custom-call | tf_op jit(solution)/shard_map/ffn_block/pallas_call | solution.py:420
  132.3 1.7 %copy.21 = bf16[64,2560]{1,0:T(8,128)(2,1)} copy(bf16[64,2560]{1,0:T(8,128)(2,1)} %ffn_block.1) | data formatting | bytes 655360

commit v4 on v0

v4 whole, which is shorter than its diff:
```python
import jax
import jax.numpy as jnp
from jax import lax
from jax.experimental import pallas as pl
from jax.experimental.pallas import tpu as pltpu
from jax.sharding import PartitionSpec as P

EPS = 1e-06

MESH_ID = pl.DeviceIdType.MESH
RING = 4
SUB = 32
HALF = 16
CAP = 16
PEERS = 2 * RING * RING
PART = 16
SPAN = RING * SUB
ORDER = (2, 1, 3, 0)


def normed(values_in, gain_vec):
    return (
        values_in
        * lax.rsqrt(jnp.mean(values_in * values_in, axis=-1, keepdims=True) + EPS)
        * gain_vec
    )


def layer_kernel(
    states_ref,
    attn_gain_ref,
    query_gain_ref,
    key_gain_ref,
    segment_ref,
    prefix_ref,
    owner_ref,
    post_gain_ref,
    ffw_gain_ref,
    last_gain_ref,
    query_w_ref,
    key_w_ref,
    value_w_ref,
    keys_ref,
    values_ref,
    out_w_ref,
    gate_ref,
    up_ref,
    down_ref,
    out_ref,
    query_w,
    key_w,
    value_w,
    stored_keys,
    stored_values,
    outgoing,
    incoming,
    results,
    back,
    out_w,
    projected,
    layer_out,
    layer_opposite,
    layer_merged,
    layer_side,
    residual,
    rows_buf,
    gate_up,
    down_w,
    partial,
    opposite_in,
    merged_out,
    side_in,
    row_sum,
    send2,
    opposite_in2,
    merged_out2,
    side_in2,
    local_sem,
    query_send_sem,
    query_recv_sem,
    back_send_sem,
    back_recv_sem,
    weight_send,
    weight_recv,
    send_sem,
    recv_sem,
):
    me = lax.axis_index("req")
    layer = lax.axis_index("mlp")
    core = lax.rem(me, 2)
    chip = me // 2
    row, col = chip // RING, lax.rem(chip, RING)
    rows, width = states_ref.shape
    head = query_gain_ref.shape[1]
    heads = query_w.shape[1] // head
    cols = heads * head
    hidden = gate_ref.shape[0]
    quarter = 2 * SUB
    score_scale = head ** (-0.5)
    f32, bf16 = jnp.float32, jnp.bfloat16

    def shifted(offset, sign=1):
        down, across, flip = offset // (2 * RING), (offset // 2) % RING, offset % 2
        if sign < 0:
            down, across = (RING - down) % RING, (RING - across) % RING
        row_at = lax.rem(row + down, RING)
        col_at = lax.rem(col + across, RING)
        core_at = 1 - core if flip else core
        return ((row_at * RING + col_at) * 2 + core_at, layer)

    right, left, sibling = shifted(2), shifted(2, -1), shifted(1)
    upper, lower = shifted(2 * RING), shifted(2 * RING, -1)
    above = (me, lax.rem(layer + 1, RING))
    below = (me, lax.rem(layer + RING - 1, RING))

    barrier = pltpu.get_barrier_semaphore()
    for offset in range(1, PEERS):
        pl.semaphore_signal(barrier, inc=1, device_id=shifted(offset), device_id_type=MESH_ID)
    for peer in (above, below):
        pl.semaphore_signal(barrier, inc=1, device_id=peer, device_id_type=MESH_ID)

    sources = (gate_ref, up_ref, down_ref)
    targets = (
        gate_up.at[pl.ds(0, hidden)],
        gate_up.at[pl.ds(2 * hidden, hidden)],
        down_w.at[pl.ds(0, hidden)],
    )
    far_targets = (
        gate_up.at[pl.ds(hidden, hidden)],
        gate_up.at[pl.ds(3 * hidden, hidden)],
        down_w.at[pl.ds(hidden, hidden)],
    )
    local = []
    for index, (src, dst) in enumerate(
        (
            (query_w_ref, query_w),
            (key_w_ref, key_w),
            (value_w_ref, value_w),
            (keys_ref, stored_keys),
            (values_ref, stored_values),
            (out_w_ref, out_w),
        )
        + tuple(zip(sources, targets))
    ):
        copy = pltpu.make_async_copy(src, dst, local_sem.at[index])
        copy.start()
        local.append(copy)

    def line(ref):
        return jnp.concatenate([ref[i : i + 1] for i in range(ref.shape[0])], axis=1)

    normalized = normed(states_ref[...].astype(f32), line(attn_gain_ref)).astype(bf16)

    def column(values):
        return jnp.transpose(jnp.broadcast_to(values, (128, rows)))[:, :1]

    prefix_row = prefix_ref[...].astype(f32)
    prefix_col = column(prefix_row)
    row_at = lax.broadcasted_iota(jnp.int32, (rows, rows), 0)
    col_at = lax.broadcasted_iota(jnp.int32, (rows, rows), 1)
    same = jnp.where(
        (prefix_col == prefix_row) & (((row_at >> 3) & 1) == ((col_at >> 3) & 1)), 1.0, 0.0
    )
    rank_col = jnp.sum(jnp.where(col_at < row_at, same, 0.0), axis=1, keepdims=True)
    rank_row = jnp.sum(jnp.where(row_at < col_at, same, 0.0), axis=0, keepdims=True)
    groups = owner_ref.shape[1]
    onehot = prefix_col == lax.broadcasted_iota(jnp.int32, (rows, groups), 1).astype(f32)
    owner_col = jnp.sum(jnp.where(onehot, owner_ref[...].astype(f32), 0.0), axis=1, keepdims=True)
    owner_row = jnp.transpose(jnp.broadcast_to(owner_col, (rows, 128)))[:1]

    def place(owner, rank):
        owner = owner.astype(jnp.int32)
        down = ((owner >> 3) - row) & 3
        across = (((owner >> 1) & 3) - col) & 3
        flip = ((owner & 1) - core) & 1
        return (down * 8 + across * 2 + flip) * CAP + rank.astype(jnp.int32)

    place_col = place(owner_col, rank_col)
    place_row = place(owner_row, rank_row)
    set_row = (lax.broadcasted_iota(jnp.int32, (1, rows), 1) >> 3) & 1

    def of_set(values, group):
        count, lanes = values.shape
        return values.reshape(count // 16, 2, 8, lanes)[:, group].reshape(count // 2, lanes)

    local[0].wait()
    raw = jnp.dot(normalized, query_w[...], preferred_element_type=f32)
    queries = [
        normed(raw[:, g * head : (g + 1) * head], query_gain_ref[...]).astype(bf16)
        for g in range(heads)
    ]
    query_rows = jnp.concatenate(queries, axis=1)
    pl.semaphore_wait(barrier, PEERS + 1)
    slot_at = lax.broadcasted_iota(jnp.int32, (PART * CAP, rows), 0)
    for group in range(2):
        goal = jnp.where(set_row == group, place_row, -1)
        for part in range(PEERS // PART):
            placing = jnp.where(slot_at + part * PART * CAP == goal, 1.0, 0.0).astype(bf16)
            packed = jnp.dot(placing, query_rows, preferred_element_type=f32).astype(bf16)
            packed = packed.reshape(PART, CAP, cols)
            if part == 0:
                incoming[group, 0] = packed[0]
            outgoing[group, pl.ds(part * PART, PART)] = packed
            for offset in range(max(part * PART, 1), (part + 1) * PART):
                pltpu.make_async_remote_copy(
                    src_ref=outgoing.at[group, offset],
                    dst_ref=incoming.at[group, offset],
                    send_sem=query_send_sem.at[group],
                    recv_sem=query_recv_sem.at[group, part],
                    device_id=shifted(offset),
                    device_id_type=MESH_ID,
                ).start()
    weight_copies = []
    for index, (src, dst) in enumerate(zip(sources, far_targets)):
        copy = pltpu.make_async_remote_copy(
            src_ref=src,
            dst_ref=dst,
            send_sem=weight_send.at[index],
            recv_sem=weight_recv.at[index],
            device_id=sibling,
            device_id_type=MESH_ID,
        )
        copy.start()
        weight_copies.append(copy)

    local[1].wait()
    local[2].wait()
    raw = jnp.dot(normalized, key_w[...], preferred_element_type=f32)
    keys = normed(raw, key_gain_ref[...]).astype(bf16)
    values = jnp.dot(normalized, value_w[...], preferred_element_type=f32).astype(bf16)
    segment_row = segment_ref[...].astype(f32)
    allowed = (column(segment_row) == segment_row) & (row_at >= col_at)

    def attend(query, key, value, mask):
        scores = (
            lax.dot_general(query, key, (((1,), (1,)), ((), ())), preferred_element_type=f32)
            * score_scale
        )
        if mask is not None:
            scores = jnp.where(mask, scores, -jnp.inf)
        row_max = jnp.max(scores, axis=-1, keepdims=True)
        powers = jnp.exp(scores - row_max)
        total = jnp.sum(powers, axis=-1, keepdims=True)
        weights = (powers / total).astype(bf16)
        mixed = jnp.dot(weights, value, preferred_element_type=f32)
        return mixed, row_max + jnp.log(total)

    suffix = [attend(query, keys, values, allowed) for query in queries]

    def remote_blocks(buf, group, part):
        start = max(part * PART, 1)
        return buf.at[group, pl.ds(start, (part + 1) * PART - start)]

    def await_blocks(buf, group, part, sem):
        blocks = remote_blocks(buf, group, part)
        pltpu.make_async_copy(blocks, blocks, sem).wait()

    local[3].wait()
    local[4].wait()
    lanes = lax.broadcasted_iota(jnp.int32, (PART * CAP, 128), 1)
    for group in range(2):
        for part in range(PEERS // PART):
            await_blocks(incoming, group, part, query_recv_sem.at[group, part])
            blocks = pl.ds(part * PART, PART)
            query = incoming[group, blocks].reshape(PART * CAP, cols)
            tail = jnp.zeros((PART * CAP, 128), f32)
            for g in range(heads):
                mixed, log_total = attend(
                    query[:, g * head : (g + 1) * head], stored_keys[...], stored_values[...], None
                )
                coarse = log_total.astype(bf16).astype(f32)
                tail = jnp.where(lanes == 2 * g, coarse, tail)
                tail = jnp.where(lanes == 2 * g + 1, log_total - coarse, tail)
                results[group, blocks, :, pl.ds(g * head, head)] = mixed.astype(bf16).reshape(
                    PART, CAP, head
                )
            results[group, blocks, :, pl.ds(cols, 128)] = tail.astype(bf16).reshape(
                PART, CAP, 128
            )
            if part == 0:
                back[group, 0] = results[group, 0]
            for offset in range(max(part * PART, 1), (part + 1) * PART):
                pltpu.make_async_remote_copy(
                    src_ref=results.at[group, offset],
                    dst_ref=back.at[group, offset],
                    send_sem=back_send_sem.at[group],
                    recv_sem=back_recv_sem.at[group, part],
                    device_id=shifted(offset, -1),
                    device_id_type=MESH_ID,
                ).start()

    copies = []

    def send(src, dst, peer):
        index = len(copies)
        copy = pltpu.make_async_remote_copy(
            src_ref=src,
            dst_ref=dst,
            send_sem=send_sem.at[index],
            recv_sem=recv_sem.at[index],
            device_id=peer,
            device_id_type=MESH_ID,
        )
        copy.start()
        copies.append(copy)
        return copy

    def quarter_rows(ref, group, offset, start, size):
        at = lax.rem(layer + offset, RING) * SUB + start
        return ref.at[group, pl.ds(pl.multiple_of(at, HALF), size)]

    layer_opp, layer_plain, layer_far = {}, {}, {}

    def project(group):
        picked = jnp.zeros((rows // 2, cols + 128), f32)
        places = of_set(place_col, group)
        for part in range(PEERS // PART):
            await_blocks(back, group, part, back_recv_sem.at[group, part])
            slots = lax.broadcasted_iota(jnp.int32, (rows // 2, PART * CAP), 1)
            choosing = jnp.where(slots + part * PART * CAP == places, 1.0, 0.0).astype(bf16)
            block = back[group, pl.ds(part * PART, PART)].reshape(PART * CAP, cols + 128)
            picked = picked + jnp.dot(choosing, block, preferred_element_type=f32)
        attended = []
        for g in range(heads):
            mixed, log_total = suffix[g]
            at = cols + 2 * g
            prefix_lse = picked[:, at : at + 1] + picked[:, at + 1 : at + 2]
            blend = jax.nn.sigmoid(prefix_lse - of_set(log_total, group))
            attended.append(
                (
                    blend * picked[:, g * head : (g + 1) * head]
                    + (1.0 - blend) * of_set(mixed, group)
                ).astype(bf16)
            )
        out = jnp.dot(jnp.concatenate(attended, axis=1), out_w[...], preferred_element_type=f32)
        projected[group] = out
        layer_out[group] = out.astype(bf16)
        layer_opp[group] = (
            send(quarter_rows(layer_out, group, 2, 0, HALF), layer_opposite.at[0, group], above),
            send(quarter_rows(layer_out, group, 2, HALF, HALF), layer_opposite.at[1, group], below),
        )
        layer_plain[group] = (
            send(
                quarter_rows(layer_out, group, 1, HALF, HALF),
                layer_side.at[0, group, pl.ds(HALF, HALF)],
                above,
            ),
            send(
                quarter_rows(layer_out, group, 3, 0, HALF),
                layer_side.at[1, group, pl.ds(0, HALF)],
                below,
            ),
        )

    def merge_layers(group):
        layer_opp[group][0].wait_recv()
        layer_merged[0, group] = (
            quarter_rows(projected, group, 1, 0, HALF)[...] + layer_opposite[0, group].astype(f32)
        ).astype(bf16)
        a = send(layer_merged.at[0, group], layer_side.at[0, group, pl.ds(0, HALF)], above)
        layer_opp[group][1].wait_recv()
        layer_merged[1, group] = (
            quarter_rows(projected, group, 3, HALF, HALF)[...]
            + layer_opposite[1, group].astype(f32)
        ).astype(bf16)
        b = send(layer_merged.at[1, group], layer_side.at[1, group, pl.ds(HALF, HALF)], below)
        layer_far[group] = (a, b)

    first = ((right, left), (upper, lower))
    second = ((upper, lower), (right, left))
    step1, step2, across, relays = {}, {}, {}, {}

    def slot(group, chunk, sub, start=0, size=SUB):
        return rows_buf.at[chunk, pl.ds(group * SPAN + sub * SUB + start, size)]

    def send_across(group, sub):
        plus, minus = second[group]
        across[group, sub] = (
            send(slot(group, 0, sub), slot(group, 3, sub), plus),
            send(slot(group, 0, sub), slot(group, 1, sub), minus),
        )

    def relay_across(group, sub):
        plus, minus = second[group]
        across[group, sub][0].wait_recv()
        a = send(slot(group, 3, sub, 0, HALF), slot(group, 2, sub, 0, HALF), plus)
        across[group, sub][1].wait_recv()
        b = send(slot(group, 1, sub, HALF, HALF), slot(group, 2, sub, HALF, HALF), minus)
        relays[group, sub] = (a, b)

    def enter(group):
        for copy in layer_plain[group] + layer_far[group]:
            copy.wait_recv()
        total = (
            quarter_rows(projected, group, 0, 0, SUB)[...]
            + layer_side[0, group].astype(f32)
            + layer_side[1, group].astype(f32)
        )
        own = states_ref[pl.ds(pl.multiple_of(layer * quarter, quarter), quarter)].astype(f32)
        after = of_set(own, group) + normed(total, line(post_gain_ref))
        residual[group] = after
        rows_buf[0, pl.ds(group * SPAN, SUB)] = normed(after, line(ffw_gain_ref)).astype(bf16)
        plus, minus = first[group]
        step1[group] = (
            send(slot(group, 0, 0), slot(group, 0, 3), plus),
            send(slot(group, 0, 0), slot(group, 0, 1), minus),
        )
        send_across(group, 0)

    def spread(group):
        plus, minus = first[group]
        step1[group][0].wait_recv()
        a = send(slot(group, 0, 3, 0, HALF), slot(group, 0, 2, 0, HALF), plus)
        step1[group][1].wait_recv()
        b = send(slot(group, 0, 1, HALF, HALF), slot(group, 0, 2, HALF, HALF), minus)
        step2[group] = (a, b)
        send_across(group, 1)
        send_across(group, 3)

    def finish_spread(group):
        for copy in step2[group]:
            copy.wait_recv()
        send_across(group, 2)

    def compute(chunk, start, size):
        span = pl.ds(start, size)
        both = lax.dot_general(
            rows_buf[chunk, span],
            gate_up[...],
            (((1,), (1,)), ((), ())),
            preferred_element_type=f32,
        )
        gate = both[:, : 2 * hidden]
        act = (jax.nn.gelu(gate, approximate=True) * both[:, 2 * hidden :]).astype(bf16)
        partial[chunk, span] = jnp.dot(act, down_w[...], preferred_element_type=f32).astype(bf16)

    local[5].wait()
    project(0)
    merge_layers(0)
    project(1)
    enter(0)
    merge_layers(1)
    spread(0)
    relay_across(0, 0)
    enter(1)
    finish_spread(0)
    spread(1)
    relay_across(0, 1)
    relay_across(0, 3)
    relay_across(1, 0)
    finish_spread(1)
    for copy in local[6:]:
        copy.wait()
    for copy in weight_copies:
        copy.wait_recv()
    relay_across(0, 2)
    relay_across(1, 1)
    relay_across(1, 3)
    compute(0, 0, 2 * SPAN)
    relay_across(1, 2)
    compute(1, 0, 2 * SPAN)
    compute(3, 0, 2 * SPAN)

    opposite, plain, merged, last = {}, {}, {}, {}

    def piece(group, chunk, sub, start):
        return partial.at[chunk, pl.ds(group * SPAN + sub * SUB + start, HALF)]

    def side(group, which, sub, start):
        return side_in.at[which, group, sub, pl.ds(start, HALF)]

    def send_opposite(group):
        plus, minus = second[group]
        for sub in ORDER:
            opposite[group, sub] = (
                send(piece(group, 2, sub, 0), opposite_in.at[0, group, sub], plus),
                send(piece(group, 2, sub, HALF), opposite_in.at[1, group, sub], minus),
            )

    def send_plain(group):
        plus, minus = second[group]
        for sub in ORDER:
            plain[group, sub] = (
                send(piece(group, 1, sub, HALF), side(group, 0, sub, HALF), plus),
                send(piece(group, 3, sub, 0), side(group, 1, sub, 0), minus),
            )

    def merge(group, sub):
        plus, minus = second[group]
        opposite[group, sub][0].wait_recv()
        merged_out[0, group, sub] = (
            piece(group, 1, sub, 0)[...].astype(f32) + opposite_in[0, group, sub].astype(f32)
        ).astype(bf16)
        a = send(merged_out.at[0, group, sub], side(group, 0, sub, 0), plus)
        opposite[group, sub][1].wait_recv()
        merged_out[1, group, sub] = (
            piece(group, 3, sub, HALF)[...].astype(f32) + opposite_in[1, group, sub].astype(f32)
        ).astype(bf16)
        b = send(merged_out.at[1, group, sub], side(group, 1, sub, HALF), minus)
        merged[group, sub] = (a, b)

    def summed(group, sub):
        for copy in plain[group, sub] + merged[group, sub]:
            copy.wait_recv()
        return (
            partial[0, pl.ds(group * SPAN + sub * SUB, SUB)].astype(f32)
            + side_in[0, group, sub].astype(f32)
            + side_in[1, group, sub].astype(f32)
        )

    def turn_opposite(group):
        plus, minus = first[group]
        send2[group, 2] = summed(group, 2).astype(bf16)
        last[group, 0] = send(
            send2.at[group, 2, pl.ds(0, HALF)], opposite_in2.at[group, 0], plus
        )
        last[group, 1] = send(
            send2.at[group, 2, pl.ds(HALF, HALF)], opposite_in2.at[group, 1], minus
        )

    def turn_side(group, which):
        sub = (1, 3)[which]
        start = (HALF, 0)[which]
        row_sum[group, which] = summed(group, sub)
        send2[group, sub] = row_sum[group, which].astype(bf16)
        last[group, 2 + which] = send(
            send2.at[group, sub, pl.ds(start, HALF)],
            side_in2.at[group, which, pl.ds(start, HALF)],
            first[group][which],
        )

    def turn_merge(group, which):
        start = (0, HALF)[which]
        last[group, which].wait_recv()
        merged_out2[group, which] = (
            row_sum[group, which, pl.ds(start, HALF)] + opposite_in2[group, which].astype(f32)
        ).astype(bf16)
        last[group, 4 + which] = send(
            merged_out2.at[group, which],
            side_in2.at[group, which, pl.ds(start, HALF)],
            first[group][which],
        )

    def finish(group):
        own = summed(group, 0)
        for index in (2, 3, 4, 5):
            last[group, index].wait_recv()
        total = own + side_in2[group, 0].astype(f32) + side_in2[group, 1].astype(f32)
        return residual[group] + normed(total, line(last_gain_ref))

    send_plain(0)
    for sub in range(RING):
        relays[0, sub][0].wait_recv()
        relays[0, sub][1].wait_recv()
    compute(2, 0, SPAN)
    send_opposite(0)
    send_plain(1)
    for sub in range(RING):
        relays[1, sub][0].wait_recv()
        relays[1, sub][1].wait_recv()
    compute(2, SPAN, SPAN)
    send_opposite(1)
    for sub in ORDER:
        merge(0, sub)
    for sub in ORDER:
        merge(1, sub)
    for group in range(2):
        turn_opposite(group)
        turn_side(group, 0)
        turn_side(group, 1)
        turn_merge(group, 0)
        turn_merge(group, 1)
    ends = [finish(group).reshape(RING, 1, 8, width) for group in range(2)]
    out_ref[...] = jnp.concatenate(ends, axis=1).reshape(quarter, width).astype(out_ref.dtype)

    for group in range(2):
        for buf, sem in ((outgoing, query_send_sem), (results, back_send_sem)):
            blocks = buf.at[group, pl.ds(1, PEERS - 1)]
            pltpu.make_async_copy(blocks, blocks, sem.at[group]).wait()
    for copy in copies + weight_copies:
        copy.wait_send()


def body(
    states,
    attn_gain,
    query_matrix,
    key_matrix,
    value_matrix,
    query_gain,
    key_gain,
    out_weight,
    post_gain,
    ffw_gain,
    gate_weight,
    up_weight,
    down_weight,
    post_ffw_gain,
    prefix_key_cache,
    prefix_value_cache,
    segment,
    prefix_id,
    owner_map,
):
    rows, width = states.shape
    cols = query_matrix.shape[1]
    hidden = gate_weight.shape[1]
    keys, values = prefix_key_cache[0], prefix_value_cache[0]
    vmem = pl.BlockSpec(memory_space=pltpu.VMEM)
    hbm = pl.BlockSpec(memory_space=pl.ANY)
    f32, bf16 = jnp.float32, jnp.bfloat16
    links = 112
    dma = pltpu.SemaphoreType.DMA
    return pl.pallas_call(
        layer_kernel,
        out_shape=jax.ShapeDtypeStruct((2 * SUB, width), bf16),
        in_specs=[vmem] * 10 + [hbm] * 9,
        out_specs=vmem,
        scratch_shapes=[
            pltpu.VMEM(query_matrix.shape, bf16),
            pltpu.VMEM(key_matrix.shape, bf16),
            pltpu.VMEM(value_matrix.shape, bf16),
            pltpu.VMEM(keys.shape, bf16),
            pltpu.VMEM(values.shape, bf16),
            pltpu.VMEM((2, PEERS, CAP, cols), bf16),
            pltpu.VMEM((2, PEERS, CAP, cols), bf16),
            pltpu.VMEM((2, PEERS, CAP, cols + 128), bf16),
            pltpu.VMEM((2, PEERS, CAP, cols + 128), bf16),
            pltpu.VMEM(out_weight.shape, bf16),
            pltpu.VMEM((2, SPAN, width), f32),
            pltpu.VMEM((2, SPAN, width), bf16),
            pltpu.VMEM((2, 2, HALF, width), bf16),
            pltpu.VMEM((2, 2, HALF, width), bf16),
            pltpu.VMEM((2, 2, SUB, width), bf16),
            pltpu.VMEM((2, SUB, width), f32),
            pltpu.VMEM((RING, 2 * SPAN, width), bf16),
            pltpu.VMEM((4 * hidden, width), bf16),
            pltpu.VMEM((2 * hidden, width), bf16),
            pltpu.VMEM((RING, 2 * SPAN, width), bf16),
            pltpu.VMEM((2, 2, RING, HALF, width), bf16),
            pltpu.VMEM((2, 2, RING, HALF, width), bf16),
            pltpu.VMEM((2, 2, RING, SUB, width), bf16),
            pltpu.VMEM((2, 2, SUB, width), f32),
            pltpu.VMEM((2, RING, SUB, width), bf16),
            pltpu.VMEM((2, 2, HALF, width), bf16),
            pltpu.VMEM((2, 2, HALF, width), bf16),
            pltpu.VMEM((2, 2, SUB, width), bf16),
            dma((9,)),
            dma((2,)),
            dma((2, 2)),
            dma((2,)),
            dma((2, 2)),
            dma((3,)),
            dma((3,)),
            dma((links,)),
            dma((links,)),
        ],
        compiler_params=pltpu.CompilerParams(
            collective_id=0, has_side_effects=True, vmem_limit_bytes=60 << 20
        ),
        name="layer",
    )(
        states,
        attn_gain.reshape(-1, 128),
        query_gain[None],
        key_gain[None],
        segment[None],
        prefix_id[None],
        owner_map[None],
        post_gain.reshape(-1, 128),
        ffw_gain.reshape(-1, 128),
        post_ffw_gain.reshape(-1, 128),
        query_matrix,
        key_matrix,
        value_matrix,
        keys,
        values,
        out_weight,
        gate_weight.T,
        up_weight.T,
        down_weight,
    )


def solution(mesh):
    return jax.shard_map(
        body,
        mesh=mesh,
        in_specs=(
            P("req", None),
            P(),
            P(None, "mlp"),
            P(None, "mlp"),
            P(None, "mlp"),
            P(),
            P(),
            P("mlp", None),
            P(),
            P(),
            P(None, "req"),
            P(None, "req"),
            P("req", None),
            P(),
            P("req", None, "mlp"),
            P("req", None, "mlp"),
            P("req"),
            P("req"),
            P(),
        ),
        out_specs=P(("req", "mlp"), None),
        check_vma=False,
    )
```

time: 343 us -> 123 us (0.36)
  waiting for transfers between devices: 228 us -> 0 us
  Pallas kernels: 0 us -> 121 us
  matrix products: 44.8 us -> 0 us
  other arithmetic: 19.4 us -> 0 us
  starting transfers between devices: 19.1 us -> 0 us
  local copies, waits for them, and re-layouts: 17.5 us -> 1.72 us
  between operations: 13.4 us -> 0.01 us
    pallas_call x0 -> x1, Pallas kernels: none -> 121 us  [body(): pl.pallas_call(layer_kernel, out_shape=jax.ShapeDtypeStruct((2 * SUB, wid...]
    reduce_scatter x1 -> x0, waiting for transfers between devices: 97.7 us -> none  [body(): lax.psum_scatter(jnp.dot(hidden, down_weight, preferred_element_type=jnp....]
    all_gather x1 -> x0, waiting for transfers between devices: 58.3 us -> none  [body(): piece = lax.all_gather(ffw_in, 'req', axis=0, tiled=True)]
    dot_general x11 -> x0, matrix products: 44.8 us -> none  [the longest x1 15.6 us: body(): jnp.dot(hidden, down_weight, preferred_element_type=jnp.float32)]
    psum x1 -> x0, waiting for transfers between devices: 43.6 us -> none  [body(): lax.psum(partial_value.astype(jnp.bfloat16), 'mlp').astype(jnp.float32)]
    all_to_all x3 -> x0, waiting for transfers between devices: 28.7 us -> none  [the longest x1 14.8 us: body(): lax.all_to_all(mixed.astype(jnp.bfloat16), 'req', split_axis=0, concat_ax...]
    all_to_all x3 -> x0, starting transfers between devices: 18.8 us -> none  [the longest x1 7.53 us: body(): lax.all_to_all(outgoing, 'req', split_axis=0, concat_axis=0, tiled=True)]
    convert_element_type x5 -> x0, other arithmetic: 8.78 us -> none  [the longest x1 3.16 us: body(): states_f = states.astype(jnp.float32)]
  transfers between devices with their start and end apart: 6 -> 0, of which waited for: 5 -> 0; matrix products, arithmetic and copies ran while one was open for 5% -> 0% of each run, Pallas kernels for 0% -> 0%
where the time goes in v4:
time: 123 us; the launch traced here: 122 us
  Pallas kernels  121 us (98%)
  local copies, waits for them, and re-layouts  1.72 us (1%)
    pallas_call x1, Pallas kernels, body(): pl.pallas_call(layer_kernel, out_shape=jax.ShapeDtypeStruct((2 * SUB, wid...  121 us

profile of v4, /device:TPU:0, one launch (start us, length us, event | category | flops | bytes accessed | tf_op | source)
XLA Modules:
  0.0 122.5 jit_solution(11103202984343212680)
XLA Ops:
  0.0 120.8 %layer.1 = bf16[64,2560]{1,0:T(8,128)(2,1)} custom-call(bf16[256,2560]{1,0:T(8,128)(2,1)} %states_ref.1, f32[20,128]{1,0:T(8,128)} %bitcast.17, f32[1,256]{1,0:T(1,128)} %bitcast.21, f32[1,256]{1,0:T(1,128)} %bitcast.22, s32[1,256]{1,0:T(1,128)} %bitcast.23, s32[1,256]{1,0:T(1,128)} %bitcast.24, s32[1,32]{1,0:T(1,128)} %bitcast.25, f32[20,128]{1,0:T(8,128)} %bitcast.18, ...), custom_call_target="tpu_custom_call" | custom-call | tf_op jit(solution)/shard_map/layer/pallas_call | solution.py:614
  120.8 1.7 %copy.21 = bf16[64,2560]{1,0:T(8,128)(2,1)} copy(bf16[64,2560]{1,0:T(8,128)(2,1)} %layer.1) | data formatting | bytes 655360

commit v5 on v4

--- a/solution.py
+++ b/solution.py
@@ -192,7 +192,7 @@
     query_rows = jnp.concatenate(queries, axis=1)
     pl.semaphore_wait(barrier, PEERS + 1)
     slot_at = lax.broadcasted_iota(jnp.int32, (PART * CAP, rows), 0)
-    for group in range(2):
+    def send_queries(group):
         goal = jnp.where(set_row == group, place_row, -1)
         for part in range(PEERS // PART):
             placing = jnp.where(slot_at + part * PART * CAP == goal, 1.0, 0.0).astype(bf16)
@@ -210,6 +210,8 @@
                     device_id=shifted(offset),
                     device_id_type=MESH_ID,
                 ).start()
+
+    send_queries(0)
     weight_copies = []
     for index, (src, dst) in enumerate(zip(sources, far_targets)):
         copy = pltpu.make_async_remote_copy(
@@ -246,6 +248,7 @@
         return mixed, row_max + jnp.log(total)
 
     suffix = [attend(query, keys, values, allowed) for query in queries]
+    send_queries(1)
 
     def remote_blocks(buf, group, part):
         start = max(part * PART, 1)
@@ -258,7 +261,7 @@
     local[3].wait()
     local[4].wait()
     lanes = lax.broadcasted_iota(jnp.int32, (PART * CAP, 128), 1)
-    for group in range(2):
+    def answer(group):
         for part in range(PEERS // PART):
             await_blocks(incoming, group, part, query_recv_sem.at[group, part])
             blocks = pl.ds(part * PART, PART)
@@ -277,6 +280,9 @@
             results[group, blocks, :, pl.ds(cols, 128)] = tail.astype(bf16).reshape(
                 PART, CAP, 128
             )
+
+    def send_answers(group):
+        for part in range(PEERS // PART):
             if part == 0:
                 back[group, 0] = results[group, 0]
             for offset in range(max(part * PART, 1), (part + 1) * PART):
@@ -288,6 +294,14 @@
                     device_id=shifted(offset, -1),
                     device_id_type=MESH_ID,
                 ).start()
+
+
+    answer(0)
+    send_answers(0)
+    answer(1)
+    blocks = results.at[0, pl.ds(1, PEERS - 1)]
+    pltpu.make_async_copy(blocks, blocks, back_send_sem.at[0]).wait()
+    send_answers(1)
 
     copies = []
 
@@ -437,8 +451,8 @@
     local[5].wait()
     project(0)
     merge_layers(0)
+    enter(0)
     project(1)
-    enter(0)
     merge_layers(1)
     spread(0)
     relay_across(0, 0)
@@ -562,21 +576,23 @@
     send_opposite(1)
     for sub in ORDER:
         merge(0, sub)
-    for sub in ORDER:
         merge(1, sub)
     for group in range(2):
         turn_opposite(group)
+    for group in range(2):
         turn_side(group, 0)
         turn_side(group, 1)
+    for group in range(2):
         turn_merge(group, 0)
         turn_merge(group, 1)
     ends = [finish(group).reshape(RING, 1, 8, width) for group in range(2)]
     out_ref[...] = jnp.concatenate(ends, axis=1).reshape(quarter, width).astype(out_ref.dtype)
 
     for group in range(2):
-        for buf, sem in ((outgoing, query_send_sem), (results, back_send_sem)):
-            blocks = buf.at[group, pl.ds(1, PEERS - 1)]
-            pltpu.make_async_copy(blocks, blocks, sem.at[group]).wait()
+        blocks = outgoing.at[group, pl.ds(1, PEERS - 1)]
+        pltpu.make_async_copy(blocks, blocks, query_send_sem.at[group]).wait()
+    blocks = results.at[1, pl.ds(1, PEERS - 1)]
+    pltpu.make_async_copy(blocks, blocks, back_send_sem.at[1]).wait()
     for copy in copies + weight_copies:
         copy.wait_send()
 

time: 123 us -> 117 us (0.951)
  Pallas kernels: 121 us -> 115 us
    pallas_call x1, Pallas kernels: 121 us -> 115 us  [body(): pl.pallas_call(layer_kernel, out_shape=jax.ShapeDtypeStruct((2 * SUB, wid...]
where the time goes in v5:
time: 117 us
  Pallas kernels  115 us (98%)
  local copies, waits for them, and re-layouts  1.72 us (1%)
    pallas_call x1, Pallas kernels, body(): pl.pallas_call(layer_kernel, out_shape=jax.ShapeDtypeStruct((2 * SUB, wid...  115 us

profile of v5, /device:TPU:0, one launch (start us, length us, event | category | flops | bytes accessed | tf_op | source)
XLA Modules:
  0.0 116.6 jit_solution(1960941439546015882)
XLA Ops:
  0.0 114.8 %layer.1 = bf16[64,2560]{1,0:T(8,128)(2,1)} custom-call(bf16[256,2560]{1,0:T(8,128)(2,1)} %states_ref.1, f32[20,128]{1,0:T(8,128)} %bitcast.17, f32[1,256]{1,0:T(1,128)} %bitcast.21, f32[1,256]{1,0:T(1,128)} %bitcast.22, s32[1,256]{1,0:T(1,128)} %bitcast.23, s32[1,256]{1,0:T(1,128)} %bitcast.24, s32[1,32]{1,0:T(1,128)} %bitcast.25, f32[20,128]{1,0:T(8,128)} %bitcast.18, ...), custom_call_target="tpu_custom_call" | custom-call | tf_op jit(solution)/shard_map/layer/pallas_call | solution.py:630
  114.9 1.7 %copy.21 = bf16[64,2560]{1,0:T(8,128)(2,1)} copy(bf16[64,2560]{1,0:T(8,128)(2,1)} %layer.1) | data formatting | bytes 655360

commit v6 on v5

--- a/solution.py
+++ b/solution.py
@@ -56,6 +56,8 @@
     incoming,
     results,
     back,
+    log_out,
+    log_back,
     out_w,
     projected,
     layer_out,
@@ -80,6 +82,8 @@
     query_recv_sem,
     back_send_sem,
     back_recv_sem,
+    log_send_sem,
+    log_recv_sem,
     weight_send,
     weight_recv,
     send_sem,
@@ -261,30 +265,30 @@
     local[3].wait()
     local[4].wait()
     lanes = lax.broadcasted_iota(jnp.int32, (PART * CAP, 128), 1)
+    slot_of = lax.broadcasted_iota(jnp.int32, (PART * CAP, 128), 0) & (CAP - 1)
     def answer(group):
         for part in range(PEERS // PART):
             await_blocks(incoming, group, part, query_recv_sem.at[group, part])
             blocks = pl.ds(part * PART, PART)
             query = incoming[group, blocks].reshape(PART * CAP, cols)
-            tail = jnp.zeros((PART * CAP, 128), f32)
+            totals = jnp.zeros((PART * CAP, 128), f32)
             for g in range(heads):
                 mixed, log_total = attend(
                     query[:, g * head : (g + 1) * head], stored_keys[...], stored_values[...], None
                 )
-                coarse = log_total.astype(bf16).astype(f32)
-                tail = jnp.where(lanes == 2 * g, coarse, tail)
-                tail = jnp.where(lanes == 2 * g + 1, log_total - coarse, tail)
+                totals = jnp.where(lanes == CAP * g + slot_of, log_total, totals)
                 results[group, blocks, :, pl.ds(g * head, head)] = mixed.astype(bf16).reshape(
                     PART, CAP, head
                 )
-            results[group, blocks, :, pl.ds(cols, 128)] = tail.astype(bf16).reshape(
-                PART, CAP, 128
+            log_out[group, blocks] = jnp.sum(
+                totals.reshape(PART, CAP, 128), axis=1, keepdims=True
             )
 
     def send_answers(group):
         for part in range(PEERS // PART):
             if part == 0:
                 back[group, 0] = results[group, 0]
+                log_back[group, 0] = log_out[group, 0]
             for offset in range(max(part * PART, 1), (part + 1) * PART):
                 pltpu.make_async_remote_copy(
                     src_ref=results.at[group, offset],
@@ -294,7 +298,15 @@
                     device_id=shifted(offset, -1),
                     device_id_type=MESH_ID,
                 ).start()
-
+            for offset in range(max(part * PART, 1), (part + 1) * PART):
+                pltpu.make_async_remote_copy(
+                    src_ref=log_out.at[group, offset],
+                    dst_ref=log_back.at[group, offset],
+                    send_sem=log_send_sem.at[group],
+                    recv_sem=log_recv_sem.at[group, part],
+                    device_id=shifted(offset, -1),
+                    device_id_type=MESH_ID,
+                ).start()
 
     answer(0)
     send_answers(0)
@@ -326,19 +338,31 @@
     layer_opp, layer_plain, layer_far = {}, {}, {}
 
     def project(group):
-        picked = jnp.zeros((rows // 2, cols + 128), f32)
+        picked = jnp.zeros((rows // 2, cols), f32)
         places = of_set(place_col, group)
         for part in range(PEERS // PART):
             await_blocks(back, group, part, back_recv_sem.at[group, part])
             slots = lax.broadcasted_iota(jnp.int32, (rows // 2, PART * CAP), 1)
             choosing = jnp.where(slots + part * PART * CAP == places, 1.0, 0.0).astype(bf16)
-            block = back[group, pl.ds(part * PART, PART)].reshape(PART * CAP, cols + 128)
+            block = back[group, pl.ds(part * PART, PART)].reshape(PART * CAP, cols)
             picked = picked + jnp.dot(choosing, block, preferred_element_type=f32)
+            await_blocks(log_back, group, part, log_recv_sem.at[group, part])
+        peer_at = lax.broadcasted_iota(jnp.int32, (rows // 2, PEERS), 1)
+        totals = jnp.dot(
+            jnp.where(peer_at == places >> 4, 1.0, 0.0),
+            log_back[group].reshape(PEERS, 128),
+            precision=lax.Precision.HIGHEST,
+            preferred_element_type=f32,
+        )
+        lane_at = lax.broadcasted_iota(jnp.int32, (rows // 2, 128), 1)
         attended = []
         for g in range(heads):
             mixed, log_total = suffix[g]
-            at = cols + 2 * g
-            prefix_lse = picked[:, at : at + 1] + picked[:, at + 1 : at + 2]
+            prefix_lse = jnp.sum(
+                jnp.where(lane_at == CAP * g + (places & (CAP - 1)), totals, 0.0),
+                axis=1,
+                keepdims=True,
+            )
             blend = jax.nn.sigmoid(prefix_lse - of_set(log_total, group))
             attended.append(
                 (
@@ -562,18 +586,14 @@
         total = own + side_in2[group, 0].astype(f32) + side_in2[group, 1].astype(f32)
         return residual[group] + normed(total, line(last_gain_ref))
 
-    send_plain(0)
-    for sub in range(RING):
-        relays[0, sub][0].wait_recv()
-        relays[0, sub][1].wait_recv()
-    compute(2, 0, SPAN)
-    send_opposite(0)
-    send_plain(1)
-    for sub in range(RING):
-        relays[1, sub][0].wait_recv()
-        relays[1, sub][1].wait_recv()
-    compute(2, SPAN, SPAN)
-    send_opposite(1)
+    for group in range(2):
+        send_plain(group)
+    for pair in relays.values():
+        pair[0].wait_recv()
+        pair[1].wait_recv()
+    compute(2, 0, 2 * SPAN)
+    for group in range(2):
+        send_opposite(group)
     for sub in ORDER:
         merge(0, sub)
         merge(1, sub)
@@ -589,8 +609,9 @@
     out_ref[...] = jnp.concatenate(ends, axis=1).reshape(quarter, width).astype(out_ref.dtype)
 
     for group in range(2):
-        blocks = outgoing.at[group, pl.ds(1, PEERS - 1)]
-        pltpu.make_async_copy(blocks, blocks, query_send_sem.at[group]).wait()
+        for buf, sem in ((outgoing, query_send_sem), (log_out, log_send_sem)):
+            blocks = buf.at[group, pl.ds(1, PEERS - 1)]
+            pltpu.make_async_copy(blocks, blocks, sem.at[group]).wait()
     blocks = results.at[1, pl.ds(1, PEERS - 1)]
     pltpu.make_async_copy(blocks, blocks, back_send_sem.at[1]).wait()
     for copy in copies + weight_copies:
@@ -640,8 +661,10 @@
             pltpu.VMEM(values.shape, bf16),
             pltpu.VMEM((2, PEERS, CAP, cols), bf16),
             pltpu.VMEM((2, PEERS, CAP, cols), bf16),
-            pltpu.VMEM((2, PEERS, CAP, cols + 128), bf16),
-            pltpu.VMEM((2, PEERS, CAP, cols + 128), bf16),
+            pltpu.VMEM((2, PEERS, CAP, cols), bf16),
+            pltpu.VMEM((2, PEERS, CAP, cols), bf16),
+            pltpu.VMEM((2, PEERS, 1, 128), f32),
+            pltpu.VMEM((2, PEERS, 1, 128), f32),
             pltpu.VMEM(out_weight.shape, bf16),
             pltpu.VMEM((2, SPAN, width), f32),
             pltpu.VMEM((2, SPAN, width), bf16),
@@ -662,6 +685,8 @@
             pltpu.VMEM((2, 2, HALF, width), bf16),
             pltpu.VMEM((2, 2, SUB, width), bf16),
             dma((9,)),
+            dma((2,)),
+            dma((2, 2)),
             dma((2,)),
             dma((2, 2)),
             dma((2,)),

time: 117 us -> 113 us (0.966)
  Pallas kernels: 115 us -> 111 us
    pallas_call x1, Pallas kernels: 115 us -> 111 us  [body(): pl.pallas_call(layer_kernel, out_shape=jax.ShapeDtypeStruct((2 * SUB, wid...]
where the time goes in v6:
time: 113 us; the launch traced here: 112 us
  Pallas kernels  111 us (98%)
  local copies, waits for them, and re-layouts  1.72 us (2%)
    pallas_call x1, Pallas kernels, body(): pl.pallas_call(layer_kernel, out_shape=jax.ShapeDtypeStruct((2 * SUB, wid...  111 us

profile of v6, /device:TPU:0, one launch (start us, length us, event | category | flops | bytes accessed | tf_op | source)
XLA Modules:
  0.0 112.3 jit_solution(11263682059900451701)
XLA Ops:
  0.0 110.6 %layer.1 = bf16[64,2560]{1,0:T(8,128)(2,1)} custom-call(bf16[256,2560]{1,0:T(8,128)(2,1)} %states_ref.1, f32[20,128]{1,0:T(8,128)} %bitcast.17, f32[1,256]{1,0:T(1,128)} %bitcast.21, f32[1,256]{1,0:T(1,128)} %bitcast.22, s32[1,256]{1,0:T(1,128)} %bitcast.23, s32[1,256]{1,0:T(1,128)} %bitcast.24, s32[1,32]{1,0:T(1,128)} %bitcast.25, f32[20,128]{1,0:T(8,128)} %bitcast.18, ...), custom_call_target="tpu_custom_call" | custom-call | tf_op jit(solution)/shard_map/layer/pallas_call | solution.py:651
  110.6 1.7 %copy.21 = bf16[64,2560]{1,0:T(8,128)(2,1)} copy(bf16[64,2560]{1,0:T(8,128)(2,1)} %layer.1) | data formatting | bytes 655360

commit v7 on v6

--- a/solution.py
+++ b/solution.py
@@ -16,6 +16,17 @@
 PART = 16
 SPAN = RING * SUB
 ORDER = (2, 1, 3, 0)
+
+
+def hops(offset):
+    down, across = offset // (2 * RING), (offset // 2) % RING
+    return min(down, RING - down) + min(across, RING - across)
+
+
+FAR_FIRST = [
+    sorted(range(max(start, 1), start + PART), key=lambda offset: -hops(offset))
+    for start in range(0, PEERS, PART)
+]
 
 
 def normed(values_in, gain_vec):
@@ -205,7 +216,7 @@
             if part == 0:
                 incoming[group, 0] = packed[0]
             outgoing[group, pl.ds(part * PART, PART)] = packed
-            for offset in range(max(part * PART, 1), (part + 1) * PART):
+            for offset in FAR_FIRST[part]:
                 pltpu.make_async_remote_copy(
                     src_ref=outgoing.at[group, offset],
                     dst_ref=incoming.at[group, offset],
@@ -289,7 +300,7 @@
             if part == 0:
                 back[group, 0] = results[group, 0]
                 log_back[group, 0] = log_out[group, 0]
-            for offset in range(max(part * PART, 1), (part + 1) * PART):
+            for offset in FAR_FIRST[part]:
                 pltpu.make_async_remote_copy(
                     src_ref=results.at[group, offset],
                     dst_ref=back.at[group, offset],
@@ -298,7 +309,7 @@
                     device_id=shifted(offset, -1),
                     device_id_type=MESH_ID,
                 ).start()
-            for offset in range(max(part * PART, 1), (part + 1) * PART):
+            for offset in FAR_FIRST[part]:
                 pltpu.make_async_remote_copy(
                     src_ref=log_out.at[group, offset],
                     dst_ref=log_back.at[group, offset],

time: 113 us -> 111 us (0.982)
  Pallas kernels: 111 us -> 109 us
    pallas_call x1, Pallas kernels: 111 us -> 109 us  [body(): pl.pallas_call(layer_kernel, out_shape=jax.ShapeDtypeStruct((2 * SUB, wid...]
where the time goes in v7:
time: 111 us
  Pallas kernels  109 us (98%)
  local copies, waits for them, and re-layouts  1.72 us (2%)
    pallas_call x1, Pallas kernels, body(): pl.pallas_call(layer_kernel, out_shape=jax.ShapeDtypeStruct((2 * SUB, wid...  109 us

profile of v7, /device:TPU:0, one launch (start us, length us, event | category | flops | bytes accessed | tf_op | source)
XLA Modules:
  0.0 110.9 jit_solution(15236369342581242375)
XLA Ops:
  0.0 109.1 %layer.1 = bf16[64,2560]{1,0:T(8,128)(2,1)} custom-call(bf16[256,2560]{1,0:T(8,128)(2,1)} %states_ref.1, f32[20,128]{1,0:T(8,128)} %bitcast.17, f32[1,256]{1,0:T(1,128)} %bitcast.21, f32[1,256]{1,0:T(1,128)} %bitcast.22, s32[1,256]{1,0:T(1,128)} %bitcast.23, s32[1,256]{1,0:T(1,128)} %bitcast.24, s32[1,32]{1,0:T(1,128)} %bitcast.25, f32[20,128]{1,0:T(8,128)} %bitcast.18, ...), custom_call_target="tpu_custom_call" | custom-call | tf_op jit(solution)/shard_map/layer/pallas_call | solution.py:662
  109.1 1.7 %copy.21 = bf16[64,2560]{1,0:T(8,128)(2,1)} copy(bf16[64,2560]{1,0:T(8,128)(2,1)} %layer.1) | data formatting | bytes 655360
